TPU v7x, 32 devices: a whole 2x2x4 slice. The times are simulated.
32 devices in a mesh: blk: 16 (over z, y, core), uly: 2 (over x).
Axes of the slice: x: 2, y: 2, z: 4, core: 2. Of those that a mesh axis runs over, the one named last changes fastest.
Arguments:
- tokens: bfloat16 [4096, 5120], P(('blk', 'uly')), may hold values from -6 to 6
- query_base: bfloat16 [4096, 5120], P(('blk', 'uly')), may hold values from -9 to 9
- key_base: bfloat16 [4096, 5120], P(('blk', 'uly')), may hold values from -9 to 9
- value_base: bfloat16 [4096, 5120], P(('blk', 'uly')), may hold values from -6 to 6
- out_grad: bfloat16 [4096, 5120], P(('blk', 'uly')), may hold values from -0.059814453 to 0.059814453
- down_q: bfloat16 [5120, 64], replicated, may hold values from -0.078125 to 0.078125
- up_q: bfloat16 [64, 5120], replicated, may hold values from -0.75 to 0.75
- down_v: bfloat16 [5120, 64], replicated, may hold values from -0.078125 to 0.078125
- up_v: bfloat16 [64, 5120], replicated, may hold values from -0.75 to 0.75
Outputs:
- attended: bfloat16 [4096, 5120], P(('blk', 'uly'))
- grad_down_q: bfloat16 [5120, 64], replicated
- grad_up_q: bfloat16 [64, 5120], P(None, 'uly')
- grad_down_v: bfloat16 [5120, 64], replicated
- grad_up_v: bfloat16 [64, 5120], P(None, 'uly')
All inputs are finite; a program needn't handle non-finite values.
Results may differ from a plain program's by a relative error of at most 0.025.
Values may be sent and summed in bfloat16 or wider, within the bound.
A program may use at most 128 MiB of HBM per device.

v0:
```python
import functools

import jax
import jax.numpy as jnp
from jax import lax
from jax.experimental import pallas as pl
from jax.experimental.pallas import tpu as pltpu
from jax.sharding import PartitionSpec as P

HEAD = 128
CHUNK = 512
MESH = pl.DeviceIdType.MESH
F32 = jnp.float32
BF16 = jnp.bfloat16


def inner(left, right):
    return lax.dot_general(left, right, (((0,), (0,)), ((), ())), preferred_element_type=F32)


def outer(left, right):
    return lax.dot_general(left, right, (((1,), (1,)), ((), ())), preferred_element_type=F32)


def dot(left, right):
    return jnp.dot(left, right, preferred_element_type=F32)


def attention_kernel(
    nb, nu,
    tokens, query_base, key_base, value_base, out_grad, down_q, up_q, down_v, up_v,
    att_ref, gup_ref, low_out,
    kbuf, vbuf, lbuf, tok, qs, gs, downs, ups, lrq, lrv, lrin,
    local_sem, xsend, xrecv, fsend, frecv, lsend, lrecv, msend, mrecv, rsend, rrecv,
):
    blk = lax.axis_index("blk")
    u = lax.axis_index("uly")
    rows, width = tokens.shape
    rank = up_q.shape[0]
    span = nu * rows
    chunks = width // CHUNK
    has_prev = blk > 0
    has_next = blk < nb - 1
    mine = pl.ds(pl.multiple_of(span + u * rows, rows), rows)

    def peer(j):
        return lax.rem(u + j, nu)

    def source(j):
        return lax.rem(u - j + nu, nu)

    def cols(c):
        return pl.ds(pl.multiple_of(c * CHUNK, CHUNK), CHUNK)

    barrier = pltpu.get_barrier_semaphore()
    for j in range(1, nu):
        pl.semaphore_signal(barrier, inc=1, device_id=(blk, peer(j)), device_id_type=MESH)

    @pl.when(has_prev)
    def _():
        for j in range(nu):
            pl.semaphore_signal(barrier, inc=1, device_id=(blk - 1, peer(j)), device_id_type=MESH)

    @pl.when(has_next)
    def _():
        for j in range(nu):
            pl.semaphore_signal(barrier, inc=1, device_id=(blk + 1, peer(j)), device_id_type=MESH)

    local = [
        pltpu.make_async_copy(src, dst, local_sem.at[i])
        for i, (src, dst) in enumerate(
            (
                (tokens, tok), (down_q, downs.at[pl.ds(0, rank)]), (down_v, downs.at[pl.ds(rank, rank)]),
                (up_q, ups.at[pl.ds(0, rank)]), (up_v, ups.at[pl.ds(rank, rank)]),
                (value_base, vbuf.at[mine]), (key_base, kbuf.at[mine]),
                (query_base, qs), (out_grad, gs),
            )
        )
    ]
    for copy in local:
        copy.start()

    edge = jnp.logical_or(blk == 0, blk == nb - 1)

    @pl.when(edge)
    def _():
        pl.semaphore_wait(barrier, 2 * nu - 1)

    @pl.when(jnp.logical_not(edge))
    def _():
        pl.semaphore_wait(barrier, 3 * nu - 1)

    bufs = (kbuf, vbuf)

    def across(a, j, c):
        src = key_base.at[:, cols(c)] if a == 0 else vbuf.at[mine, cols(c)]
        return pltpu.make_async_remote_copy(
            src_ref=src, dst_ref=bufs[a].at[mine, cols(c)],
            send_sem=xsend.at[a, j, c], recv_sem=xrecv.at[a, j, c],
            device_id=(blk, peer(j)), device_id_type=MESH,
        )

    def crossed(a, j, c):
        here = bufs[a].at[pl.ds(pl.multiple_of(span + source(j) * rows, rows), rows), cols(c)]
        return pltpu.make_async_remote_copy(
            src_ref=here, dst_ref=here,
            send_sem=xsend.at[a, j, c], recv_sem=xrecv.at[a, j, c],
            device_id=(blk, peer(j)), device_id_type=MESH,
        )

    def onward(a, j, c):
        s = source(j)
        if a == 0 and j == 0:
            src = key_base.at[:, cols(c)]
        else:
            src = bufs[a].at[pl.ds(pl.multiple_of(span + s * rows, rows), rows), cols(c)]
        return pltpu.make_async_remote_copy(
            src_ref=src, dst_ref=bufs[a].at[pl.ds(pl.multiple_of(s * rows, rows), rows), cols(c)],
            send_sem=fsend.at[a, j, c], recv_sem=frecv.at[a, j, c],
            device_id=(blk + 1, u), device_id_type=MESH,
        )

    def arrived(a, j, c):
        here = bufs[a].at[pl.ds(pl.multiple_of(source(j) * rows, rows), rows), cols(c)]
        return pltpu.make_async_remote_copy(
            src_ref=here, dst_ref=here,
            send_sem=fsend.at[a, j, c], recv_sem=frecv.at[a, j, c],
            device_id=(blk, peer(1)), device_id_type=MESH,
        )

    def low_across(j):
        return pltpu.make_async_remote_copy(
            src_ref=lbuf.at[mine], dst_ref=lbuf.at[mine],
            send_sem=lsend.at[j], recv_sem=lrecv.at[j],
            device_id=(blk, peer(j)), device_id_type=MESH,
        )

    def low_crossed(j):
        here = lbuf.at[pl.ds(pl.multiple_of(span + source(j) * rows, rows), rows)]
        return pltpu.make_async_remote_copy(
            src_ref=here, dst_ref=here, send_sem=lsend.at[j], recv_sem=lrecv.at[j],
            device_id=(blk, peer(j)), device_id_type=MESH,
        )

    def low_onward(j):
        s = source(j)
        return pltpu.make_async_remote_copy(
            src_ref=lbuf.at[pl.ds(pl.multiple_of(span + s * rows, rows), rows)],
            dst_ref=lbuf.at[pl.ds(pl.multiple_of(s * rows, rows), rows)],
            send_sem=msend.at[j], recv_sem=mrecv.at[j],
            device_id=(blk + 1, u), device_id_type=MESH,
        )

    def low_arrived(j):
        here = lbuf.at[pl.ds(pl.multiple_of(source(j) * rows, rows), rows)]
        return pltpu.make_async_remote_copy(
            src_ref=here, dst_ref=here, send_sem=msend.at[j], recv_sem=mrecv.at[j],
            device_id=(blk, peer(1)), device_id_type=MESH,
        )

    early = min(3, chunks)
    for c in range(early):
        for j in range(1, nu):
            across(0, j, c).start()

        @pl.when(has_next)
        def _():
            onward(0, 0, c).start()

    lane = lax.broadcasted_iota(jnp.int32, (rows, 2 * rank), 1)
    for i in range(3):
        local[i].wait()
    low = outer(tok[...], downs[...])
    low_qm = jnp.where(lane < rank, low, 0.0).astype(BF16)
    low_vm = jnp.where(lane >= rank, low, 0.0).astype(BF16)
    lbuf[mine, :] = low_vm
    for i in range(3, 6):
        local[i].wait()

    @pl.loop(0, chunks)
    def _(c):
        part = dot(low_vm, ups[:, cols(c)])
        vbuf[mine, cols(c)] = (vbuf[mine, cols(c)].astype(F32) + part).astype(BF16)

    for j in range(1, nu):
        low_across(j).start()

    @pl.when(has_next)
    def _():
        low_onward(0).start()

    @pl.loop(0, chunks)
    def _(c):
        @pl.when(c >= early)
        def _():
            for j in range(1, nu):
                across(0, j, c).start()

            @pl.when(has_next)
            def _():
                onward(0, 0, c).start()

        for j in range(1, nu):
            across(1, j, c).start()

        @pl.when(has_next)
        def _():
            onward(1, 0, c).start()

    lrq[...] = jnp.zeros_like(lrq)
    lrv[...] = jnp.zeros_like(lrv)

    @pl.when(jnp.logical_not(has_prev))
    def _():
        kbuf[pl.ds(0, span), :] = jnp.zeros((span, width), BF16)
        vbuf[pl.ds(0, span), :] = jnp.zeros((span, width), BF16)
        lbuf[pl.ds(0, span), :] = jnp.zeros((span, 2 * rank), BF16)

    for i in range(6, 9):
        local[i].wait()

    scale = HEAD ** (-0.5)
    key_at = lax.broadcasted_iota(jnp.int32, (rows, 2 * span), 1)
    usable = jnp.logical_or(key_at >= span, has_prev)

    def head(h):
        at = pl.ds(pl.multiple_of(h * HEAD, HEAD), HEAD)
        up = ups[:, at]
        keys = kbuf[:, at]
        values = vbuf[:, at]
        grad = gs[:, at]
        query = (qs[:, at].astype(F32) + dot(low_qm, up)).astype(BF16)
        scores = jnp.where(usable, outer(query, keys) * scale, -jnp.inf)
        weights = jnp.exp(scores - jnp.max(scores, axis=1, keepdims=True))
        total = jnp.sum(weights, axis=1, keepdims=True)
        probs = (weights * (1.0 / total)).astype(BF16)
        attended = dot(probs, values).astype(BF16)
        delta = jnp.sum(grad.astype(F32) * attended.astype(F32), axis=1, keepdims=True)
        score_grad = (probs.astype(F32) * (outer(grad, values) - delta)).astype(BF16)
        query_grad = (dot(score_grad, keys) * scale).astype(BF16)
        seen = dot(probs, lbuf[...]).astype(BF16)
        gup = (inner(low_qm, query_grad) + inner(seen, grad)).astype(BF16)
        lifted = jnp.where(lane >= rank, outer(grad, up), 0.0).astype(BF16)
        return attended, gup, outer(query_grad, up), inner(probs, lifted)

    together = 2 if span <= 2 * HEAD else 1

    def head_group(first):
        results = [head(first + i) for i in range(together)]
        for i, (attended, gup, _, _) in enumerate(results):
            h = first + i
            att_ref[:, pl.ds(pl.multiple_of(h * HEAD, HEAD), HEAD)] = attended
            gup_ref[pl.ds(pl.multiple_of(h * 2 * rank, 2 * rank), 2 * rank), :] = gup
        lrq[...] += jnp.where(lane < rank, sum(r[2] for r in results), 0.0)
        lrv[...] += sum(r[3] for r in results)

    heads = CHUNK // HEAD

    @pl.loop(0, chunks + 1)
    def _(c):
        @pl.when(c == 0)
        def _():
            for j in range(1, nu):
                low_crossed(j).wait_recv()

                @pl.when(has_next)
                def _():
                    low_onward(j).start()

            @pl.when(has_prev)
            def _():
                for j in range(nu):
                    low_arrived(j).wait_recv()

        @pl.when(c < chunks)
        def _():
            for a in range(2):
                for j in range(1, nu):
                    crossed(a, j, c).wait_recv()

                    @pl.when(has_next)
                    def _():
                        onward(a, j, c).start()

        @pl.when(c > 0)
        def _():
            @pl.when(has_prev)
            def _():
                for a in range(2):
                    for j in range(nu):
                        arrived(a, j, c - 1).wait_recv()

            @pl.loop(0, heads // together)
            def _(i):
                head_group((c - 1) * heads + i * together)

    def terms(k, j, base):
        s = peer(j)
        return pltpu.make_async_remote_copy(
            src_ref=lrv.at[pl.ds(pl.multiple_of(base + s * rows, rows), rows)],
            dst_ref=lrin.at[k, j],
            send_sem=rsend.at[k, j], recv_sem=rrecv.at[k, j],
            device_id=(blk - k, s), device_id_type=MESH,
        )

    for j in range(1, nu):
        terms(0, j, span).start()

    @pl.when(has_prev)
    def _():
        for j in range(nu):
            terms(1, j, 0).start()

    @pl.loop(0, chunks)
    def _(c):
        for a in range(2):
            for j in range(1, nu):
                across(a, j, c).wait_send()

            @pl.when(has_next)
            def _():
                for j in range(nu):
                    onward(a, j, c).wait_send()

    for j in range(1, nu):
        low_across(j).wait_send()

    @pl.when(has_next)
    def _():
        for j in range(nu):
            low_onward(j).wait_send()

    lrq[...] += lrv[mine, :]
    for j in range(1, nu):
        terms(0, j, span).wait_recv()
        lrq[...] += lrin[0, j]

    @pl.when(has_next)
    def _():
        for j in range(nu):
            terms(1, j, 0).wait_recv()
            lrq[...] += lrin[1, j]

    low_out[...] = lrq[...].astype(BF16)
    for j in range(1, nu):
        terms(0, j, span).wait_send()

    @pl.when(has_prev)
    def _():
        for j in range(nu):
            terms(1, j, 0).wait_send()


def attention(nb, nu, *operands):
    rows, width = operands[0].shape
    rank = operands[6].shape[0]
    span = nu * rows
    chunks = width // CHUNK
    dma = pltpu.SemaphoreType.DMA
    anywhere = pl.BlockSpec(memory_space=pl.ANY)
    here = pl.BlockSpec(memory_space=pltpu.VMEM)
    return pl.pallas_call(
        functools.partial(attention_kernel, nb, nu),
        out_shape=(
            jax.ShapeDtypeStruct((rows, width), BF16),
            jax.ShapeDtypeStruct((width // HEAD * 2 * rank, HEAD), BF16),
            jax.ShapeDtypeStruct((rows, 2 * rank), BF16),
        ),
        in_specs=[anywhere] * 9,
        out_specs=(here, here, here),
        scratch_shapes=[
            pltpu.VMEM((2 * span, width), BF16),
            pltpu.VMEM((2 * span, width), BF16),
            pltpu.VMEM((2 * span, 2 * rank), BF16),
            pltpu.VMEM((rows, width), BF16),
            pltpu.VMEM((rows, width), BF16),
            pltpu.VMEM((rows, width), BF16),
            pltpu.VMEM((2 * rank, width), BF16),
            pltpu.VMEM((2 * rank, width), BF16),
            pltpu.VMEM((rows, 2 * rank), F32),
            pltpu.VMEM((2 * span, 2 * rank), F32),
            pltpu.VMEM((2, nu, rows, 2 * rank), F32),
            dma((9,)),
            dma((2, nu, chunks)), dma((2, nu, chunks)),
            dma((2, nu, chunks)), dma((2, nu, chunks)),
            dma((nu,)), dma((nu,)), dma((nu,)), dma((nu,)),
            dma((2, nu)), dma((2, nu)),
        ],
        compiler_params=pltpu.CompilerParams(
            collective_id=0, has_side_effects=True, vmem_limit_bytes=65_000_000
        ),
    )(*operands)


def reduction_kernel(
    nb, nu,
    tokens, lowrank, gup,
    downq_out, downv_out, upq_out, upv_out,
    tok, terms, pair, part, plane_in, line, line_in, down, ups, flat,
    local_sem, psend, precv, asend, arecv, bsend, brecv, csend, crecv, dsend, drecv, esend, erecv,
):
    blk = lax.axis_index("blk")
    u = lax.axis_index("uly")
    core = lax.rem(blk, 2)
    chip = blk // 2
    other = chip * 2 + 1 - core
    half = nb // 2
    inners = plane_in.shape[1] // nu
    outers = half // inners
    y = lax.rem(chip, inners)
    z = chip // inners
    group = nu * inners
    rows, width = tokens.shape
    rank = upq_out.shape[0]
    region = pair.shape[2]
    sub = plane_in.shape[2]
    piece = line_in.shape[2]

    def split(o, sign):
        pu = lax.rem(u + sign * (o // inners) + nu, nu)
        py = lax.rem(y + sign * lax.rem(o, inners) + inners, inners)
        return pu, py

    def plane_dev(o):
        pu, py = split(o, 1)
        return ((z * inners + py) * 2 + core, pu)

    def peer_z(o):
        return lax.rem(z + o, outers)

    def from_z(o):
        return lax.rem(z - o + outers, outers)

    def line_dev(o):
        return ((peer_z(o) * inners + y) * 2 + core, u)

    def subs(p):
        return pl.ds(pl.multiple_of(p * sub, sub), sub)

    barrier = pltpu.get_barrier_semaphore()
    pl.semaphore_signal(barrier, inc=1, device_id=(other, u), device_id_type=MESH)
    for o in range(1, group):
        pl.semaphore_signal(barrier, inc=1, device_id=plane_dev(o), device_id_type=MESH)
    for o in range(1, outers):
        pl.semaphore_signal(barrier, inc=1, device_id=line_dev(o), device_id_type=MESH)

    load = pltpu.make_async_copy(tokens, tok, local_sem.at[0])
    load.start()
    pl.semaphore_wait(barrier, group + outers - 1)

    def remote(src, dst, send, recv, device):
        return pltpu.make_async_remote_copy(
            src_ref=src, dst_ref=dst, send_sem=send, recv_sem=recv,
            device_id=device, device_id_type=MESH,
        )

    def swap(t, v):
        rows_at = pl.ds(pl.multiple_of((v * 2 + 1 - core) * region, region), region)
        return remote(
            (terms if t == 0 else gup).at[rows_at], pair.at[t, v],
            psend.at[t, v], precv.at[t, v], (other, u),
        )

    def scatter(t, o):
        pu, py = split(o, 1)
        return remote(
            part.at[t, pu, subs(py)], plane_in.at[t, o],
            asend.at[t, o], arecv.at[t, o], plane_dev(o),
        )

    def pass_on(t, o):
        at = pl.ds(pl.multiple_of(peer_z(o) * piece, piece), piece)
        return remote(
            line.at[t, at], line_in.at[t, o], bsend.at[t, o], brecv.at[t, o], line_dev(o)
        )

    def whole(t, v, k, p):
        return down.at[v, k, subs(p)] if t == 0 else ups.at[k, subs(p)]

    def piece_at(p, q):
        return pl.ds(pl.multiple_of(p * sub + q * piece, piece), piece)

    def small(t, q):
        return down.at[u, core, piece_at(y, q)] if t == 0 else ups.at[core, piece_at(y, q)]

    def along(t, o):
        return remote(small(t, z), small(t, z), csend.at[t, o], crecv.at[t, o], line_dev(o))

    def came(t, o):
        here = small(t, from_z(o))
        return remote(here, here, csend.at[t, o], crecv.at[t, o], line_dev(o))

    def spread(t, o):
        here = whole(t, u, core, y)
        return remote(here, here, dsend.at[t, o], drecv.at[t, o], plane_dev(o))

    def landed(t, o):
        pu, py = split(o, -1)
        here = whole(t, pu, core, py)
        return remote(here, here, dsend.at[t, o], drecv.at[t, o], (other, u))

    def share(t, o):
        pu, py = split(o, -1)
        here = whole(t, pu, core, py)
        return remote(here, here, esend.at[t, o], erecv.at[t, o], (other, u))

    def shared(t, o):
        pu, py = split(o, -1)
        here = whole(t, pu, 1 - core, py)
        return remote(here, here, esend.at[t, o], erecv.at[t, o], (other, u))

    if part.shape[2] > region:
        part[...] = jnp.zeros_like(part)
    for v in range(nu):
        swap(1, v).start()

    load.wait()
    lows = lowrank[...]

    @pl.loop(0, width // HEAD)
    def _(h):
        cols = pl.ds(pl.multiple_of(h * HEAD, HEAD), HEAD)
        here = pl.ds(pl.multiple_of(h * 2 * rank, 2 * rank), 2 * rank)
        terms[here, :] = inner(lows, tok[:, cols]).astype(BF16)

    for v in range(nu):
        swap(0, v).start()

    for t in (1, 0):
        for v in range(nu):
            rows_at = pl.ds(pl.multiple_of((v * 2 + core) * region, region), region)
            own = (terms if t == 0 else gup)[rows_at, :]
            swap(t, v).wait_recv()
            part[t, v, pl.ds(0, region), :] = (
                own.astype(F32) + pair[t, v].astype(F32)
            ).astype(BF16)
        for o in range(1, group):
            scatter(t, o).start()

    for t in (1, 0):
        total = part[t, u, subs(y), :].astype(F32)
        for o in range(1, group):
            scatter(t, o).wait_recv()
            total = total + plane_in[t, o].astype(F32)
        line[t, :, :] = total.astype(BF16)
        for o in range(1, outers):
            pass_on(t, o).start()

    for t in (1, 0):
        total = line[t, pl.ds(pl.multiple_of(z * piece, piece), piece), :].astype(F32)
        for o in range(1, outers):
            pass_on(t, o).wait_recv()
            total = total + line_in[t, o].astype(F32)
        small(t, z)[...] = total.astype(BF16)
        for o in range(1, outers):
            along(t, o).start()

    counts = (group, inners)
    for t in (1, 0):
        for o in range(1, outers):
            came(t, o).wait_recv()
        for o in range(1, counts[t]):
            spread(t, o).start()
        share(t, 0).start()

    for t in (1, 0):
        for o in range(1, counts[t]):
            landed(t, o).wait_recv()
            share(t, o).start()

    for t in (1, 0):
        for o in range(counts[t]):
            shared(t, o).wait_recv()
        places = [(v, k) for v in range(nu if t == 0 else 1) for k in range(2)]
        for n, (v, k) in enumerate(places):
            flat[pl.ds(n * region, region), :] = (
                down[v, k, pl.ds(0, region), :] if t == 0 else ups[k, pl.ds(0, region), :]
            )
        outs = (downq_out, downv_out) if t == 0 else (upq_out, upv_out)
        for h in range(len(places) * region // (2 * rank)):
            cols = pl.ds(h * HEAD, HEAD)
            outs[0][:, cols] = flat[pl.ds(h * 2 * rank, rank), :]
            outs[1][:, cols] = flat[pl.ds(h * 2 * rank + rank, rank), :]

    for t in (1, 0):
        for v in range(nu):
            swap(t, v).wait_send()
        for o in range(1, group):
            scatter(t, o).wait_send()
        for o in range(1, outers):
            pass_on(t, o).wait_send()
            along(t, o).wait_send()
        for o in range(1, counts[t]):
            spread(t, o).wait_send()
        for o in range(counts[t]):
            share(t, o).wait_send()


def reduction(nb, nu, tokens, lowrank, gup):
    rows, width = tokens.shape
    rank = lowrank.shape[1] // 2
    half = nb // 2
    inners = 2 if half % 2 == 0 else 1
    outers = half // inners
    group = nu * inners
    region = width // (2 * nu)
    piece = -(-region // (16 * half)) * 16
    sub = outers * piece
    held = half * piece
    dma = pltpu.SemaphoreType.DMA
    here = pl.BlockSpec(memory_space=pltpu.VMEM)
    lanes = lowrank.shape[1]
    return pl.pallas_call(
        functools.partial(reduction_kernel, nb, nu),
        out_shape=(
            jax.ShapeDtypeStruct((rank, width), BF16),
            jax.ShapeDtypeStruct((rank, width), BF16),
            jax.ShapeDtypeStruct((rank, width // nu), BF16),
            jax.ShapeDtypeStruct((rank, width // nu), BF16),
        ),
        in_specs=[pl.BlockSpec(memory_space=pl.ANY), here, here],
        out_specs=(here, here, here, here),
        scratch_shapes=[
            pltpu.VMEM((rows, width), BF16),
            pltpu.VMEM((width, lanes), BF16),
            pltpu.VMEM((2, nu, region, lanes), BF16),
            pltpu.VMEM((2, nu, held, lanes), BF16),
            pltpu.VMEM((2, group, sub, lanes), BF16),
            pltpu.VMEM((2, sub, lanes), BF16),
            pltpu.VMEM((2, outers, piece, lanes), BF16),
            pltpu.VMEM((nu, 2, held, lanes), BF16),
            pltpu.VMEM((2, held, lanes), BF16),
            pltpu.VMEM((2 * nu * region, lanes), BF16),
            dma((1,)),
            dma((2, nu)), dma((2, nu)),
            dma((2, group)), dma((2, group)),
            dma((2, outers)), dma((2, outers)),
            dma((2, outers)), dma((2, outers)),
            dma((2, group)), dma((2, group)),
            dma((2, group)), dma((2, group)),
        ],
        compiler_params=pltpu.CompilerParams(collective_id=1, has_side_effects=True),
    )(tokens, lowrank, gup)


def per_device(nb, nu, tokens, query_base, key_base, value_base, out_grad, down_q, up_q, down_v, up_v):
    attended, gup, lowrank = attention(
        nb, nu, tokens, query_base, key_base, value_base, out_grad, down_q.T, up_q, down_v.T, up_v
    )
    grad_down_q, grad_down_v, grad_up_q, grad_up_v = reduction(nb, nu, tokens, lowrank, gup)
    return attended, grad_down_q.T, grad_up_q, grad_down_v.T, grad_up_v


def solution(mesh):
    split = P(("blk", "uly"), None)
    return jax.shard_map(
        functools.partial(per_device, mesh.shape["blk"], mesh.shape["uly"]),
        mesh=mesh,
        in_specs=(split,) * 5 + (P(),) * 4,
        out_specs=(split, P(), P(None, "uly"), P(), P(None, "uly")),
        check_vma=False,
    )
```

profile of v0, /device:TPU:9, one launch (start us, length us, event | category | flops | bytes accessed | tf_op | source)
XLA Modules:
  0.0 143.2 jit_solution(13349011079200315883)
XLA Ops:
  0.6 83.3 %shard_map.128 = (bf16[128,5120]{1,0:T(8,128)(2,1)}, bf16[5120,128]{1,0:T(8,128)(2,1)}, bf16[128,128]{1,0:T(8,128)(2,1)}) custom-call(bf16[128,5120]{1,0:T(8,128)(2,1)} %tokens.3, bf16[128,5120]{1,0:T(8,128)(2,1)} %query_base.1, bf16[128,5120]{1,0:T(8,128)(2,1)} %key_base.1, bf16[128,5120]{1,0:T(8,128)(2,1)} %value_base.1, bf16[128,5120]{1,0:T(8,128)(2,1)} %out_grad.1, ...), custom_call_target="tpu_custom_call" | custom-call | tf_op jit(solution)/shard_map/pallas_call | solution.py:362
  84.0 0.0 copy-start
  84.0 54.3 %shard_map.129 = (bf16[64,5120]{1,0:T(8,128)(2,1)}, bf16[64,5120]{1,0:T(8,128)(2,1)}, bf16[64,2560]{1,0:T(8,128)(2,1)}, bf16[64,2560]{1,0:T(8,128)(2,1)}) custom-call(bf16[128,5120]{1,0:T(8,128)(2,1)} %tokens.3, bf16[128,128]{1,0:T(8,128)(2,1)} %get-tuple-element.13.lowrank, bf16[5120,128]{1,0:T(8,128)(2,1)} %get-tuple-element.14.gup), custom_call_target="tpu_custom_call" | custom-call | tf_op jit(solution)/shard_map/pallas_call | solution.py:613
  138.3 0.0 copy-done
  138.3 0.0 copy-start.2
  138.3 1.1 copy.19
  139.3 0.4 copy-done.2
  139.8 0.0 copy-start.4
  139.8 0.0 copy-start.1
  139.8 0.8 copy.20
  140.6 0.3 copy-done.4
  140.9 0.0 copy-start.3
  140.9 0.7 copy.21
  141.7 0.0 copy-done.1
  141.7 0.8 copy.22
  142.5 0.0 copy-done.3
  142.5 0.7 copy.23
Async XLA Ops:
  84.0 54.3 %copy-start = (bf16[128,5120]{1,0:T(8,128)(2,1)S(1)}, bf16[128,5120]{1,0:T(8,128)(2,1)}, u32[]{:S(2)}) copy-start(bf16[128,5120]{1,0:T(8,128)(2,1)} %get-tuple-element.24) | copy-start | bytes 3932164
  138.3 1.5 %copy-start.2 = (bf16[64,5120]{1,0:T(8,128)(2,1)S(1)}, bf16[64,5120]{1,0:T(8,128)(2,1)}, u32[]{:S(2)}) copy-start(bf16[64,5120]{1,0:T(8,128)(2,1)} %get-tuple-element.15) | copy-start | bytes 1966084
  139.8 1.2 copy-start.4
  139.8 1.9 %copy-start.1 = (bf16[64,5120]{1,0:T(8,128)(2,1)S(1)}, bf16[64,5120]{1,0:T(8,128)(2,1)}, u32[]{:S(2)}) copy-start(bf16[64,5120]{1,0:T(8,128)(2,1)} %get-tuple-element.17) | copy-start | bytes 1966084
  140.9 1.6 %copy-start.3 = (bf16[64,2560]{1,0:T(8,128)(2,1)S(1)}, bf16[64,2560]{1,0:T(8,128)(2,1)}, u32[]{:S(2)}) copy-start(bf16[64,2560]{1,0:T(8,128)(2,1)} %get-tuple-element.28) | copy-start | bytes 983044
where the time goes:
time: 144 us; the launch traced here: 143 us
  Pallas kernels  138 us (96%)
  local copies, waits for them, and re-layouts  4.96 us (3%)
    pallas_call x1, Pallas kernels, attention(): pl.pallas_call(functools.partial(attention_kernel, nb, nu), out_shape=(ja...  83.3 us
    pallas_call x1, Pallas kernels, reduction(): pl.pallas_call(functools.partial(reduction_kernel, nb, nu), out_shape=(ja...  54.3 us
    unnamed x15, local copies, waits for them, and re-layouts  4.96 us

commit v1 on v0

--- a/solution.py
+++ b/solution.py
@@ -8,7 +8,7 @@
 from jax.sharding import PartitionSpec as P
 
 HEAD = 128
-CHUNK = 512
+CHUNK = 256
 MESH = pl.DeviceIdType.MESH
 F32 = jnp.float32
 BF16 = jnp.bfloat16
@@ -158,13 +158,15 @@
             device_id=(blk, peer(1)), device_id_type=MESH,
         )
 
-    early = min(3, chunks)
+    early = min(3 * 512 // CHUNK, chunks)
+    ahead = min(2048 // CHUNK, chunks)
     for c in range(early):
         for j in range(1, nu):
             across(0, j, c).start()
 
-        @pl.when(has_next)
-        def _():
+    @pl.when(has_next)
+    def _():
+        for c in range(ahead):
             onward(0, 0, c).start()
 
     lane = lax.broadcasted_iota(jnp.int32, (rows, 2 * rank), 1)
@@ -196,15 +198,12 @@
             for j in range(1, nu):
                 across(0, j, c).start()
 
-            @pl.when(has_next)
-            def _():
-                onward(0, 0, c).start()
-
         for j in range(1, nu):
             across(1, j, c).start()
 
-        @pl.when(has_next)
-        def _():
+    @pl.when(has_next)
+    def _():
+        for c in range(ahead):
             onward(1, 0, c).start()
 
     lrq[...] = jnp.zeros_like(lrq)
@@ -281,6 +280,11 @@
                     @pl.when(has_next)
                     def _():
                         onward(a, j, c).start()
+
+            @pl.when(jnp.logical_and(has_next, c + ahead < chunks))
+            def _():
+                for a in range(2):
+                    onward(a, 0, c + ahead).start()
 
         @pl.when(c > 0)
         def _():

time: 144 us -> 137 us (0.951)
  Pallas kernels: 138 us -> 131 us
    pallas_call x1, Pallas kernels: 83.3 us -> 77.7 us  [attention(): pl.pallas_call(functools.partial(attention_kernel, nb, nu), out_shape=(ja...]
where the time goes in v1:
time: 137 us
  Pallas kernels  131 us (96%)
  local copies, waits for them, and re-layouts  4.96 us (4%)
    pallas_call x1, Pallas kernels, attention(): pl.pallas_call(functools.partial(attention_kernel, nb, nu), out_shape=(ja...  77.7 us
    pallas_call x1, Pallas kernels, reduction(): pl.pallas_call(functools.partial(reduction_kernel, nb, nu), out_shape=(ja...  53.6 us
    unnamed x15, local copies, waits for them, and re-layouts  4.96 us

profile of v1, /device:TPU:9, one launch (start us, length us, event | category | flops | bytes accessed | tf_op | source)
XLA Modules:
  0.0 137.0 jit_solution(6823238900772410969)
XLA Ops:
  0.6 77.7 %shard_map.128 = (bf16[128,5120]{1,0:T(8,128)(2,1)}, bf16[5120,128]{1,0:T(8,128)(2,1)}, bf16[128,128]{1,0:T(8,128)(2,1)}) custom-call(bf16[128,5120]{1,0:T(8,128)(2,1)} %tokens.3, bf16[128,5120]{1,0:T(8,128)(2,1)} %query_base.1, bf16[128,5120]{1,0:T(8,128)(2,1)} %key_base.1, bf16[128,5120]{1,0:T(8,128)(2,1)} %value_base.1, bf16[128,5120]{1,0:T(8,128)(2,1)} %out_grad.1, ...), custom_call_target="tpu_custom_call" | custom-call | tf_op jit(solution)/shard_map/pallas_call | solution.py:366
  78.4 0.0 copy-start
  78.4 53.6 %shard_map.129 = (bf16[64,5120]{1,0:T(8,128)(2,1)}, bf16[64,5120]{1,0:T(8,128)(2,1)}, bf16[64,2560]{1,0:T(8,128)(2,1)}, bf16[64,2560]{1,0:T(8,128)(2,1)}) custom-call(bf16[128,5120]{1,0:T(8,128)(2,1)} %tokens.3, bf16[128,128]{1,0:T(8,128)(2,1)} %get-tuple-element.13.lowrank, bf16[5120,128]{1,0:T(8,128)(2,1)} %get-tuple-element.14.gup), custom_call_target="tpu_custom_call" | custom-call | tf_op jit(solution)/shard_map/pallas_call | solution.py:617
  132.0 0.0 copy-done
  132.0 0.0 copy-start.2
  132.1 1.1 copy.19
  133.1 0.4 copy-done.2
  133.6 0.0 copy-start.4
  133.6 0.0 copy-start.1
  133.6 0.8 copy.20
  134.4 0.3 copy-done.4
  134.7 0.0 copy-start.3
  134.7 0.7 copy.21
  135.4 0.0 copy-done.1
  135.4 0.8 copy.22
  136.3 0.0 copy-done.3
  136.3 0.7 copy.23
Async XLA Ops:
  78.4 53.7 %copy-start = (bf16[128,5120]{1,0:T(8,128)(2,1)S(1)}, bf16[128,5120]{1,0:T(8,128)(2,1)}, u32[]{:S(2)}) copy-start(bf16[128,5120]{1,0:T(8,128)(2,1)} %get-tuple-element.24) | copy-start | bytes 3932164
  132.0 1.5 %copy-start.2 = (bf16[64,5120]{1,0:T(8,128)(2,1)S(1)}, bf16[64,5120]{1,0:T(8,128)(2,1)}, u32[]{:S(2)}) copy-start(bf16[64,5120]{1,0:T(8,128)(2,1)} %get-tuple-element.15) | copy-start | bytes 1966084
  133.6 1.2 copy-start.4
  133.6 1.9 %copy-start.1 = (bf16[64,5120]{1,0:T(8,128)(2,1)S(1)}, bf16[64,5120]{1,0:T(8,128)(2,1)}, u32[]{:S(2)}) copy-start(bf16[64,5120]{1,0:T(8,128)(2,1)} %get-tuple-element.17) | copy-start | bytes 1966084
  134.7 1.6 %copy-start.3 = (bf16[64,2560]{1,0:T(8,128)(2,1)S(1)}, bf16[64,2560]{1,0:T(8,128)(2,1)}, u32[]{:S(2)}) copy-start(bf16[64,2560]{1,0:T(8,128)(2,1)} %get-tuple-element.28) | copy-start | bytes 983044

commit v2 on v1

--- a/solution.py
+++ b/solution.py
@@ -647,10 +647,638 @@
     )(tokens, lowrank, gup)
 
 
+def fused_kernel(
+    nb, nu,
+    tokens, query_base, key_base, value_base, out_grad, down_q, up_q, down_v, up_v,
+    att_out, downq_out, downv_out, upq_out, upv_out,
+    kbuf, vbuf, lbuf, tok, qs, gs, downs, ups, lrq, lrv, lrin, att_ref,
+    acc, pair, part, plane_in, line, line_in, res,
+    local_sem, att_sem, xsend, xrecv, fsend, frecv, lsend, lrecv, msend, mrecv, rsend, rrecv,
+    psend, precv, asend, arecv, bsend, brecv, csend, crecv, dsend, drecv, esend, erecv,
+):
+    blk = lax.axis_index("blk")
+    u = lax.axis_index("uly")
+    rows, width = tokens.shape
+    rank = up_q.shape[0]
+    span = nu * rows
+    chunks = width // CHUNK
+    has_prev = blk > 0
+    has_next = blk < nb - 1
+    mine = pl.ds(pl.multiple_of(span + u * rows, rows), rows)
+
+    def peer(j):
+        return lax.rem(u + j, nu)
+
+    def source(j):
+        return lax.rem(u - j + nu, nu)
+
+    cells = 2 * nu
+    parts = chunks // cells
+    core = lax.rem(blk, 2)
+    chip = blk // 2
+    other = chip * 2 + 1 - core
+    inners, outers = grid_of(nb)
+    group = nu * inners
+    y = lax.rem(chip, inners)
+    z = chip // inners
+    sub = CHUNK // inners
+    piece = sub // outers
+
+    def place(c):
+        return lax.rem(c, cells) * parts + c // cells
+
+    def cols(c):
+        return pl.ds(pl.multiple_of(place(c) * CHUNK, CHUNK), CHUNK)
+
+    def remote(src, dst, send, recv, device):
+        return pltpu.make_async_remote_copy(
+            src_ref=src, dst_ref=dst, send_sem=send, recv_sem=recv,
+            device_id=device, device_id_type=MESH,
+        )
+
+    def split(o, sign):
+        pu = lax.rem(u + sign * (o // inners) + nu, nu)
+        py = lax.rem(y + sign * lax.rem(o, inners) + inners, inners)
+        return pu, py
+
+    def plane_dev(o):
+        pu, py = split(o, 1)
+        return ((z * inners + py) * 2 + core, pu)
+
+    def peer_z(o):
+        return lax.rem(z + o, outers)
+
+    def from_z(o):
+        return lax.rem(z - o + outers, outers)
+
+    def line_dev(o):
+        return ((peer_z(o) * inners + y) * 2 + core, u)
+
+    def subs(p):
+        return pl.ds(pl.multiple_of(p * sub, sub), sub)
+
+    def piece_at(p, q):
+        return pl.ds(pl.multiple_of(p * sub + q * piece, piece), piece)
+
+    def swap(n, v):
+        return remote(
+            acc.at[n, v * 2 + 1 - core], pair.at[n, v],
+            psend.at[n, v], precv.at[n, v], (other, u),
+        )
+
+    def scatter(n, o):
+        pu, py = split(o, 1)
+        return remote(
+            part.at[n, pu, subs(py)], plane_in.at[n, o],
+            asend.at[n, o], arecv.at[n, o], plane_dev(o),
+        )
+
+    def pass_on(n, o):
+        at = pl.ds(pl.multiple_of(peer_z(o) * piece, piece), piece)
+        return remote(
+            line.at[n, at], line_in.at[n, o], bsend.at[n, o], brecv.at[n, o], line_dev(o)
+        )
+
+    def along(n, o):
+        here = res.at[n, u * 2 + core, piece_at(y, z)]
+        return remote(here, here, csend.at[n, o], crecv.at[n, o], line_dev(o))
+
+    def came(n, o):
+        here = res.at[n, u * 2 + core, piece_at(y, from_z(o))]
+        return remote(here, here, csend.at[n, o], crecv.at[n, o], line_dev(o))
+
+    def spread(n, o):
+        here = res.at[n, u * 2 + core, subs(y)]
+        return remote(here, here, dsend.at[n, o], drecv.at[n, o], plane_dev(o))
+
+    def landed(n, o):
+        pu, py = split(o, -1)
+        here = res.at[n, pu * 2 + core, subs(py)]
+        return remote(here, here, dsend.at[n, o], drecv.at[n, o], (other, u))
+
+    def share(n, o):
+        pu, py = split(o, -1)
+        here = res.at[n, pu * 2 + core, subs(py)]
+        return remote(here, here, esend.at[n, o], erecv.at[n, o], (other, u))
+
+    def shared(n, o):
+        pu, py = split(o, -1)
+        here = res.at[n, pu * 2 + 1 - core, subs(py)]
+        return remote(here, here, esend.at[n, o], erecv.at[n, o], (other, u))
+
+    def pair_up(n):
+        for v in range(nu):
+            own = acc[n, v * 2 + core]
+            swap(n, v).wait_recv()
+            part[n, v] = (own.astype(F32) + pair[n, v].astype(F32)).astype(BF16)
+        for o in range(1, group):
+            scatter(n, o).start()
+
+    def plane_sum(n):
+        total = part[n, u, subs(y), :].astype(F32)
+        for o in range(1, group):
+            scatter(n, o).wait_recv()
+            total = total + plane_in[n, o].astype(F32)
+        line[n] = total.astype(BF16)
+        for o in range(1, outers):
+            pass_on(n, o).start()
+
+    def line_sum(n):
+        total = line[n, pl.ds(pl.multiple_of(z * piece, piece), piece), :].astype(F32)
+        for o in range(1, outers):
+            pass_on(n, o).wait_recv()
+            total = total + line_in[n, o].astype(F32)
+        res[n, u * 2 + core, piece_at(y, z), :] = total.astype(BF16)
+        for o in range(1, outers):
+            along(n, o).start()
+
+    def widen(n, count):
+        for o in range(1, outers):
+            came(n, o).wait_recv()
+        for o in range(1, count):
+            spread(n, o).start()
+        share(n, 0).start()
+
+    def hand_over(n, count):
+        for o in range(1, count):
+            landed(n, o).wait_recv()
+            share(n, o).start()
+
+    def each(first, stop, work):
+        @pl.loop(first, stop)
+        def _(n):
+            work(n)
+
+    barrier = pltpu.get_barrier_semaphore()
+    for j in range(1, nu):
+        pl.semaphore_signal(barrier, inc=1, device_id=(blk, peer(j)), device_id_type=MESH)
+
+    @pl.when(has_prev)
+    def _():
+        for j in range(nu):
+            pl.semaphore_signal(barrier, inc=1, device_id=(blk - 1, peer(j)), device_id_type=MESH)
+
+    @pl.when(has_next)
+    def _():
+        for j in range(nu):
+            pl.semaphore_signal(barrier, inc=1, device_id=(blk + 1, peer(j)), device_id_type=MESH)
+
+    for o in range(1, group):
+        pl.semaphore_signal(barrier, inc=1, device_id=plane_dev(o), device_id_type=MESH)
+    for o in range(1, outers):
+        pl.semaphore_signal(barrier, inc=1, device_id=line_dev(o), device_id_type=MESH)
+
+    local = [
+        pltpu.make_async_copy(src, dst, local_sem.at[i])
+        for i, (src, dst) in enumerate(
+            (
+                (tokens, tok), (down_q, downs.at[pl.ds(0, rank)]), (down_v, downs.at[pl.ds(rank, rank)]),
+                (up_q, ups.at[pl.ds(0, rank)]), (up_v, ups.at[pl.ds(rank, rank)]),
+                (value_base, vbuf.at[mine]), (key_base, kbuf.at[mine]),
+                (query_base, qs), (out_grad, gs),
+            )
+        )
+    ]
+    for copy in local:
+        copy.start()
+
+    edge = jnp.logical_or(blk == 0, blk == nb - 1)
+
+    @pl.when(edge)
+    def _():
+        pl.semaphore_wait(barrier, 2 * nu - 1 + group + outers - 2)
+
+    @pl.when(jnp.logical_not(edge))
+    def _():
+        pl.semaphore_wait(barrier, 3 * nu - 1 + group + outers - 2)
+
+    bufs = (kbuf, vbuf)
+
+    def across(a, j, c):
+        src = key_base.at[:, cols(c)] if a == 0 else vbuf.at[mine, cols(c)]
+        return pltpu.make_async_remote_copy(
+            src_ref=src, dst_ref=bufs[a].at[mine, cols(c)],
+            send_sem=xsend.at[a, j, c], recv_sem=xrecv.at[a, j, c],
+            device_id=(blk, peer(j)), device_id_type=MESH,
+        )
+
+    def crossed(a, j, c):
+        here = bufs[a].at[pl.ds(pl.multiple_of(span + source(j) * rows, rows), rows), cols(c)]
+        return pltpu.make_async_remote_copy(
+            src_ref=here, dst_ref=here,
+            send_sem=xsend.at[a, j, c], recv_sem=xrecv.at[a, j, c],
+            device_id=(blk, peer(j)), device_id_type=MESH,
+        )
+
+    def onward(a, j, c):
+        s = source(j)
+        if a == 0 and j == 0:
+            src = key_base.at[:, cols(c)]
+        else:
+            src = bufs[a].at[pl.ds(pl.multiple_of(span + s * rows, rows), rows), cols(c)]
+        return pltpu.make_async_remote_copy(
+            src_ref=src, dst_ref=bufs[a].at[pl.ds(pl.multiple_of(s * rows, rows), rows), cols(c)],
+            send_sem=fsend.at[a, j, c], recv_sem=frecv.at[a, j, c],
+            device_id=(blk + 1, u), device_id_type=MESH,
+        )
+
+    def arrived(a, j, c):
+        here = bufs[a].at[pl.ds(pl.multiple_of(source(j) * rows, rows), rows), cols(c)]
+        return pltpu.make_async_remote_copy(
+            src_ref=here, dst_ref=here,
+            send_sem=fsend.at[a, j, c], recv_sem=frecv.at[a, j, c],
+            device_id=(blk, peer(1)), device_id_type=MESH,
+        )
+
+    def low_across(j):
+        return pltpu.make_async_remote_copy(
+            src_ref=lbuf.at[mine], dst_ref=lbuf.at[mine],
+            send_sem=lsend.at[j], recv_sem=lrecv.at[j],
+            device_id=(blk, peer(j)), device_id_type=MESH,
+        )
+
+    def low_crossed(j):
+        here = lbuf.at[pl.ds(pl.multiple_of(span + source(j) * rows, rows), rows)]
+        return pltpu.make_async_remote_copy(
+            src_ref=here, dst_ref=here, send_sem=lsend.at[j], recv_sem=lrecv.at[j],
+            device_id=(blk, peer(j)), device_id_type=MESH,
+        )
+
+    def low_onward(j):
+        s = source(j)
+        return pltpu.make_async_remote_copy(
+            src_ref=lbuf.at[pl.ds(pl.multiple_of(span + s * rows, rows), rows)],
+            dst_ref=lbuf.at[pl.ds(pl.multiple_of(s * rows, rows), rows)],
+            send_sem=msend.at[j], recv_sem=mrecv.at[j],
+            device_id=(blk + 1, u), device_id_type=MESH,
+        )
+
+    def low_arrived(j):
+        here = lbuf.at[pl.ds(pl.multiple_of(source(j) * rows, rows), rows)]
+        return pltpu.make_async_remote_copy(
+            src_ref=here, dst_ref=here, send_sem=msend.at[j], recv_sem=mrecv.at[j],
+            device_id=(blk, peer(1)), device_id_type=MESH,
+        )
+
+    early = min(3 * 512 // CHUNK, chunks)
+    ahead = min(2048 // CHUNK, chunks)
+    for c in range(early):
+        for j in range(1, nu):
+            across(0, j, c).start()
+
+    @pl.when(has_next)
+    def _():
+        for c in range(ahead):
+            onward(0, 0, c).start()
+
+    lane = lax.broadcasted_iota(jnp.int32, (rows, 2 * rank), 1)
+    for i in range(3):
+        local[i].wait()
+    low = outer(tok[...], downs[...])
+    low_qm = jnp.where(lane < rank, low, 0.0).astype(BF16)
+    low_vm = jnp.where(lane >= rank, low, 0.0).astype(BF16)
+    lbuf[mine, :] = low_vm
+    for i in range(3, 6):
+        local[i].wait()
+
+    @pl.loop(0, chunks)
+    def _(c):
+        part = dot(low_vm, ups[:, cols(c)])
+        vbuf[mine, cols(c)] = (vbuf[mine, cols(c)].astype(F32) + part).astype(BF16)
+
+    for j in range(1, nu):
+        low_across(j).start()
+
+    @pl.when(has_next)
+    def _():
+        low_onward(0).start()
+
+    @pl.loop(0, chunks)
+    def _(c):
+        @pl.when(c >= early)
+        def _():
+            for j in range(1, nu):
+                across(0, j, c).start()
+
+        for j in range(1, nu):
+            across(1, j, c).start()
+
+    @pl.when(has_next)
+    def _():
+        for c in range(ahead):
+            onward(1, 0, c).start()
+
+    lrq[...] = jnp.zeros_like(lrq)
+    lrv[...] = jnp.zeros_like(lrv)
+
+    @pl.when(jnp.logical_not(has_prev))
+    def _():
+        kbuf[pl.ds(0, span), :] = jnp.zeros((span, width), BF16)
+        vbuf[pl.ds(0, span), :] = jnp.zeros((span, width), BF16)
+        lbuf[pl.ds(0, span), :] = jnp.zeros((span, 2 * rank), BF16)
+
+    for i in range(6, 9):
+        local[i].wait()
+
+    scale = HEAD ** (-0.5)
+    key_at = lax.broadcasted_iota(jnp.int32, (rows, 2 * span), 1)
+    usable = jnp.logical_or(key_at >= span, has_prev)
+
+    def head(h):
+        at = pl.ds(pl.multiple_of(h * HEAD, HEAD), HEAD)
+        up = ups[:, at]
+        keys = kbuf[:, at]
+        values = vbuf[:, at]
+        grad = gs[:, at]
+        query = (qs[:, at].astype(F32) + dot(low_qm, up)).astype(BF16)
+        scores = jnp.where(usable, outer(query, keys) * scale, -jnp.inf)
+        weights = jnp.exp(scores - jnp.max(scores, axis=1, keepdims=True))
+        total = jnp.sum(weights, axis=1, keepdims=True)
+        probs = (weights * (1.0 / total)).astype(BF16)
+        attended = dot(probs, values).astype(BF16)
+        delta = jnp.sum(grad.astype(F32) * attended.astype(F32), axis=1, keepdims=True)
+        score_grad = (probs.astype(F32) * (outer(grad, values) - delta)).astype(BF16)
+        query_grad = (dot(score_grad, keys) * scale).astype(BF16)
+        seen = dot(probs, lbuf[...]).astype(BF16)
+        gup = (inner(low_qm, query_grad) + inner(seen, grad)).astype(BF16)
+        lifted = jnp.where(lane >= rank, outer(grad, up), 0.0).astype(BF16)
+        return attended, gup, outer(query_grad, up), inner(probs, lifted)
+
+    together = 2 if span <= 2 * HEAD else 1
+
+    def head_group(c, offset):
+        first = place(c) * heads + offset
+        results = [head(first + i) for i in range(together)]
+        for i, (attended, gup, _, _) in enumerate(results):
+            h = first + i
+            att_ref[:, pl.ds(pl.multiple_of(h * HEAD, HEAD), HEAD)] = attended
+            row = pl.multiple_of((offset + i) * 2 * rank, 2 * rank)
+            acc[c // cells, lax.rem(c, cells), pl.ds(row, 2 * rank), :] = gup
+        lrq[...] += jnp.where(lane < rank, sum(r[2] for r in results), 0.0)
+        lrv[...] += sum(r[3] for r in results)
+
+    heads = CHUNK // HEAD
+    soon = max(parts - 2, 0)
+
+    def att_copy(c):
+        return pltpu.make_async_copy(
+            att_ref.at[:, cols(c)], att_out.at[:, cols(c)], att_sem.at[c]
+        )
+
+    @pl.loop(0, chunks + 1)
+    def _(c):
+        @pl.when(c == 0)
+        def _():
+            for j in range(1, nu):
+                low_crossed(j).wait_recv()
+
+                @pl.when(has_next)
+                def _():
+                    low_onward(j).start()
+
+            @pl.when(has_prev)
+            def _():
+                for j in range(nu):
+                    low_arrived(j).wait_recv()
+
+        @pl.when(c < chunks)
+        def _():
+            for a in range(2):
+                for j in range(1, nu):
+                    crossed(a, j, c).wait_recv()
+
+                    @pl.when(has_next)
+                    def _():
+                        onward(a, j, c).start()
+
+            @pl.when(jnp.logical_and(has_next, c + ahead < chunks))
+            def _():
+                for a in range(2):
+                    onward(a, 0, c + ahead).start()
+
+        @pl.when(c == chunks - 1)
+        def _():
+            each(0, soon, pair_up)
+
+        @pl.when(c > 0)
+        def _():
+            @pl.when(has_prev)
+            def _():
+                for a in range(2):
+                    for j in range(nu):
+                        arrived(a, j, c - 1).wait_recv()
+
+            @pl.loop(0, heads // together)
+            def _(i):
+                head_group(c - 1, i * together)
+
+            att_copy(c - 1).start()
+            cell = lax.rem(c - 1, cells)
+
+            @pl.when(lax.rem(cell, 2) != core)
+            def _():
+                swap((c - 1) // cells, cell // 2).start()
+
+    def terms(k, j, base):
+        s = peer(j)
+        return pltpu.make_async_remote_copy(
+            src_ref=lrv.at[pl.ds(pl.multiple_of(base + s * rows, rows), rows)],
+            dst_ref=lrin.at[k, j],
+            send_sem=rsend.at[k, j], recv_sem=rrecv.at[k, j],
+            device_id=(blk - k, s), device_id_type=MESH,
+        )
+
+    for j in range(1, nu):
+        terms(0, j, span).start()
+
+    @pl.when(has_prev)
+    def _():
+        for j in range(nu):
+            terms(1, j, 0).start()
+
+    each(soon, parts, pair_up)
+    each(0, soon, plane_sum)
+
+    lrq[...] += lrv[mine, :]
+    for j in range(1, nu):
+        terms(0, j, span).wait_recv()
+        lrq[...] += lrin[0, j]
+
+    @pl.when(has_next)
+    def _():
+        for j in range(nu):
+            terms(1, j, 0).wait_recv()
+            lrq[...] += lrin[1, j]
+
+    lows = lrq[...].T.astype(BF16)
+
+    def terms_of(p, r):
+        at = pl.ds(pl.multiple_of((r * parts + p) * CHUNK, CHUNK), CHUNK)
+        block = dot(lows, tok[:, at]).astype(BF16)
+        for i in range(heads):
+            acc[parts + p, r, pl.ds(i * 2 * rank, 2 * rank), :] = block[:, i * HEAD:(i + 1) * HEAD]
+
+    def project(p):
+        for v in range(nu):
+            terms_of(p, v * 2 + 1 - core)
+            swap(parts + p, v).start()
+        for v in range(nu):
+            terms_of(p, v * 2 + core)
+
+    def lay_out(n, count, outs, base):
+        for o in range(count):
+            shared(n, o).wait_recv()
+        for r in range(cells if count == group else 2):
+            for i in range(heads):
+                h = (r * parts + n - base) * heads + i
+                at = pl.ds(pl.multiple_of(h * HEAD, HEAD), HEAD)
+                cell = r if count == group else u * 2 + r
+                outs[0][:, at] = res[n, cell, pl.ds(i * 2 * rank, rank), :]
+                outs[1][:, at] = res[n, cell, pl.ds(i * 2 * rank + rank, rank), :]
+
+    each(0, parts, project)
+    each(parts, 2 * parts, pair_up)
+    each(soon, parts, plane_sum)
+    each(0, parts, line_sum)
+    each(parts, 2 * parts, plane_sum)
+    each(0, parts, lambda n: widen(n, inners))
+    each(parts, 2 * parts, line_sum)
+    each(0, parts, lambda n: hand_over(n, inners))
+    each(parts, 2 * parts, lambda n: widen(n, group))
+    each(0, parts, lambda n: lay_out(n, inners, (upq_out, upv_out), 0))
+    each(parts, 2 * parts, lambda n: hand_over(n, group))
+    each(parts, 2 * parts, lambda n: lay_out(n, group, (downq_out, downv_out), parts))
+
+    def drain(n, count):
+        for v in range(nu):
+            swap(n, v).wait_send()
+        for o in range(1, group):
+            scatter(n, o).wait_send()
+        for o in range(1, outers):
+            pass_on(n, o).wait_send()
+            along(n, o).wait_send()
+        for o in range(1, count):
+            spread(n, o).wait_send()
+        for o in range(count):
+            share(n, o).wait_send()
+
+    each(0, parts, lambda n: drain(n, inners))
+    each(parts, 2 * parts, lambda n: drain(n, group))
+    each(0, chunks, lambda c: att_copy(c).wait())
+
+    @pl.loop(0, chunks)
+    def _(c):
+        for a in range(2):
+            for j in range(1, nu):
+                across(a, j, c).wait_send()
+
+            @pl.when(has_next)
+            def _():
+                for j in range(nu):
+                    onward(a, j, c).wait_send()
+
+    for j in range(1, nu):
+        low_across(j).wait_send()
+
+    @pl.when(has_next)
+    def _():
+        for j in range(nu):
+            low_onward(j).wait_send()
+
+    for j in range(1, nu):
+        terms(0, j, span).wait_send()
+
+    @pl.when(has_prev)
+    def _():
+        for j in range(nu):
+            terms(1, j, 0).wait_send()
+
+
+def grid_of(nb):
+    half = nb // 2
+    inners = 2 if half % 2 == 0 else 1
+    return inners, half // inners
+
+
+def fused(nb, nu, *operands):
+    rows, width = operands[0].shape
+    rank = operands[6].shape[0]
+    span = nu * rows
+    chunks = width // CHUNK
+    cells = 2 * nu
+    parts = chunks // cells
+    inners, outers = grid_of(nb)
+    group = nu * inners
+    sub = CHUNK // inners
+    lanes = 2 * rank
+    dma = pltpu.SemaphoreType.DMA
+    anywhere = pl.BlockSpec(memory_space=pl.ANY)
+    here = pl.BlockSpec(memory_space=pltpu.VMEM)
+    return pl.pallas_call(
+        functools.partial(fused_kernel, nb, nu),
+        out_shape=(
+            jax.ShapeDtypeStruct((rows, width), BF16),
+            jax.ShapeDtypeStruct((rank, width), BF16),
+            jax.ShapeDtypeStruct((rank, width), BF16),
+            jax.ShapeDtypeStruct((rank, width // nu), BF16),
+            jax.ShapeDtypeStruct((rank, width // nu), BF16),
+        ),
+        in_specs=[anywhere] * 9,
+        out_specs=(anywhere, here, here, here, here),
+        scratch_shapes=[
+            pltpu.VMEM((2 * span, width), BF16),
+            pltpu.VMEM((2 * span, width), BF16),
+            pltpu.VMEM((2 * span, lanes), BF16),
+            pltpu.VMEM((rows, width), BF16),
+            pltpu.VMEM((rows, width), BF16),
+            pltpu.VMEM((rows, width), BF16),
+            pltpu.VMEM((lanes, width), BF16),
+            pltpu.VMEM((lanes, width), BF16),
+            pltpu.VMEM((rows, lanes), F32),
+            pltpu.VMEM((2 * span, lanes), F32),
+            pltpu.VMEM((2, nu, rows, lanes), F32),
+            pltpu.VMEM((rows, width), BF16),
+            pltpu.VMEM((2 * parts, cells, CHUNK, lanes), BF16),
+            pltpu.VMEM((2 * parts, nu, CHUNK, lanes), BF16),
+            pltpu.VMEM((2 * parts, nu, CHUNK, lanes), BF16),
+            pltpu.VMEM((2 * parts, group, sub, lanes), BF16),
+            pltpu.VMEM((2 * parts, sub, lanes), BF16),
+            pltpu.VMEM((2 * parts, outers, sub // outers, lanes), BF16),
+            pltpu.VMEM((2 * parts, cells, CHUNK, lanes), BF16),
+            dma((9,)), dma((chunks,)),
+            dma((2, nu, chunks)), dma((2, nu, chunks)),
+            dma((2, nu, chunks)), dma((2, nu, chunks)),
+            dma((nu,)), dma((nu,)), dma((nu,)), dma((nu,)),
+            dma((2, nu)), dma((2, nu)),
+            dma((2 * parts, nu)), dma((2 * parts, nu)),
+            dma((2 * parts, group)), dma((2 * parts, group)),
+            dma((2 * parts, outers)), dma((2 * parts, outers)),
+            dma((2 * parts, outers)), dma((2 * parts, outers)),
+            dma((2 * parts, group)), dma((2 * parts, group)),
+            dma((2 * parts, group)), dma((2 * parts, group)),
+        ],
+        compiler_params=pltpu.CompilerParams(
+            collective_id=2, has_side_effects=True, vmem_limit_bytes=65_000_000
+        ),
+    )(*operands)
+
+
+def fits(nb, nu, rows, width, rank):
+    inners, outers = grid_of(nb)
+    return (
+        2 * rank == HEAD
+        and width % (2 * nu * CHUNK) == 0
+        and CHUNK % (16 * inners * outers) == 0
+        and nu * rows <= CHUNK
+    )
+
+
 def per_device(nb, nu, tokens, query_base, key_base, value_base, out_grad, down_q, up_q, down_v, up_v):
-    attended, gup, lowrank = attention(
-        nb, nu, tokens, query_base, key_base, value_base, out_grad, down_q.T, up_q, down_v.T, up_v
-    )
+    operands = (tokens, query_base, key_base, value_base, out_grad, down_q.T, up_q, down_v.T, up_v)
+    if fits(nb, nu, *tokens.shape, up_q.shape[0]):
+        attended, grad_down_q, grad_down_v, grad_up_q, grad_up_v = fused(nb, nu, *operands)
+        return attended, grad_down_q.T, grad_up_q, grad_down_v.T, grad_up_v
+    attended, gup, lowrank = attention(nb, nu, *operands)
     grad_down_q, grad_down_v, grad_up_q, grad_up_v = reduction(nb, nu, tokens, lowrank, gup)
     return attended, grad_down_q.T, grad_up_q, grad_down_v.T, grad_up_v
 

time: 137 us -> 122 us (0.89)
  Pallas kernels: 131 us -> 115 us
    pallas_call x2 -> x1, Pallas kernels: 131 us -> 115 us  [fused(): pl.pallas_call(functools.partial(fused_kernel, nb, nu), out_shape=(jax.Sh...]
    unnamed x15 -> x13, local copies, waits for them, and re-layouts: 4.96 us -> 5.95 us
where the time goes in v2:
time: 122 us
  Pallas kernels  115 us (94%)
  local copies, waits for them, and re-layouts  5.95 us (5%)
    pallas_call x1, Pallas kernels, fused(): pl.pallas_call(functools.partial(fused_kernel, nb, nu), out_shape=(jax.Sh...  115 us
    unnamed x13, local copies, waits for them, and re-layouts  5.95 us

profile of v2, /device:TPU:9, one launch (start us, length us, event | category | flops | bytes accessed | tf_op | source)
XLA Modules:
  0.0 121.7 jit_solution(7841043102365847990)
XLA Ops:
  0.6 115.1 %shard_map.128 = (bf16[128,5120]{1,0:T(8,128)(2,1)}, bf16[64,5120]{1,0:T(8,128)(2,1)}, bf16[64,5120]{1,0:T(8,128)(2,1)}, bf16[64,2560]{1,0:T(8,128)(2,1)}, bf16[64,2560]{1,0:T(8,128)(2,1)}) custom-call(bf16[128,5120]{1,0:T(8,128)(2,1)} %tokens.1, bf16[128,5120]{1,0:T(8,128)(2,1)} %query_base.1, bf16[128,5120]{1,0:T(8,128)(2,1)} %key_base.1, ...), custom_call_target="tpu_custom_call" | custom-call | tf_op jit(solution)/shard_map/pallas_call | solution.py:1217
  115.8 0.0 copy-start.1
  115.8 2.5 %copy.19 = bf16[128,5120]{1,0:T(8,128)(2,1)} copy(bf16[128,5120]{1,0:T(8,128)(2,1)} %get-tuple-element.20) | data formatting | bytes 2621440
  118.3 0.0 copy-done.1
  118.3 0.0 copy-start.3
  118.3 0.0 copy-start
  118.3 0.0 copy-start.2
  118.3 0.8 copy.20
  119.2 0.3 copy-done.3
  119.4 0.7 copy.21
  120.2 0.0 copy-done
  120.2 0.8 copy.22
  121.0 0.0 copy-done.2
  121.0 0.7 copy.23
Async XLA Ops:
  115.8 2.5 %copy-start.1 = (bf16[64,5120]{1,0:T(8,128)(2,1)S(1)}, bf16[64,5120]{1,0:T(8,128)(2,1)}, u32[]{:S(2)}) copy-start(bf16[64,5120]{1,0:T(8,128)(2,1)} %get-tuple-element.11) | copy-start | bytes 1966084
  118.3 1.1 copy-start.3
  118.3 1.9 %copy-start = (bf16[64,5120]{1,0:T(8,128)(2,1)S(1)}, bf16[64,5120]{1,0:T(8,128)(2,1)}, u32[]{:S(2)}) copy-start(bf16[64,5120]{1,0:T(8,128)(2,1)} %get-tuple-element.13) | copy-start | bytes 1966084
  118.3 2.7 %copy-start.2 = (bf16[64,2560]{1,0:T(8,128)(2,1)S(1)}, bf16[64,2560]{1,0:T(8,128)(2,1)}, u32[]{:S(2)}) copy-start(bf16[64,2560]{1,0:T(8,128)(2,1)} %get-tuple-element.24) | copy-start | bytes 983044

commit v3 on v2

--- a/solution.py
+++ b/solution.py
@@ -651,11 +651,12 @@
     nb, nu,
     tokens, query_base, key_base, value_base, out_grad, down_q, up_q, down_v, up_v,
     att_out, downq_out, downv_out, upq_out, upv_out,
-    kbuf, vbuf, lbuf, tok, qs, gs, downs, ups, lrq, lrv, lrin, att_ref,
+    kv, lbuf, tok, qs, gs, downs, ups, lrq, lrv, lrin, att_ref,
     acc, pair, part, plane_in, line, line_in, res,
     local_sem, att_sem, xsend, xrecv, fsend, frecv, lsend, lrecv, msend, mrecv, rsend, rrecv,
     psend, precv, asend, arecv, bsend, brecv, csend, crecv, dsend, drecv, esend, erecv,
 ):
+    kbuf, vbuf = kv.at[0], kv.at[1]
     blk = lax.axis_index("blk")
     u = lax.axis_index("uly")
     rows, width = tokens.shape
@@ -720,89 +721,71 @@
     def piece_at(p, q):
         return pl.ds(pl.multiple_of(p * sub + q * piece, piece), piece)
 
-    def swap(n, v):
+    def swap(n):
         return remote(
-            acc.at[n, v * 2 + 1 - core], pair.at[n, v],
-            psend.at[n, v], precv.at[n, v], (other, u),
+            acc.at[n, 1 - core], pair.at[n], psend.at[0], precv.at[n], (other, u)
         )
 
     def scatter(n, o):
         pu, py = split(o, 1)
         return remote(
-            part.at[n, pu, subs(py)], plane_in.at[n, o],
-            asend.at[n, o], arecv.at[n, o], plane_dev(o),
+            part.at[n, pu, subs(py)], plane_in.at[n, o - 1],
+            asend.at[0], arecv.at[n], plane_dev(o),
         )
 
     def pass_on(n, o):
         at = pl.ds(pl.multiple_of(peer_z(o) * piece, piece), piece)
         return remote(
-            line.at[n, at], line_in.at[n, o], bsend.at[n, o], brecv.at[n, o], line_dev(o)
+            line.at[n, at], line_in.at[n, o - 1], bsend.at[0], brecv.at[n], line_dev(o)
         )
 
     def along(n, o):
-        here = res.at[n, u * 2 + core, piece_at(y, z)]
-        return remote(here, here, csend.at[n, o], crecv.at[n, o], line_dev(o))
-
-    def came(n, o):
-        here = res.at[n, u * 2 + core, piece_at(y, from_z(o))]
-        return remote(here, here, csend.at[n, o], crecv.at[n, o], line_dev(o))
-
-    def spread(n, o):
-        here = res.at[n, u * 2 + core, subs(y)]
-        return remote(here, here, dsend.at[n, o], drecv.at[n, o], plane_dev(o))
-
-    def landed(n, o):
-        pu, py = split(o, -1)
-        here = res.at[n, pu * 2 + core, subs(py)]
-        return remote(here, here, dsend.at[n, o], drecv.at[n, o], (other, u))
-
-    def share(n, o):
-        pu, py = split(o, -1)
-        here = res.at[n, pu * 2 + core, subs(py)]
-        return remote(here, here, esend.at[n, o], erecv.at[n, o], (other, u))
-
-    def shared(n, o):
-        pu, py = split(o, -1)
-        here = res.at[n, pu * 2 + 1 - core, subs(py)]
-        return remote(here, here, esend.at[n, o], erecv.at[n, o], (other, u))
+        here = res.at[n, core, u, piece_at(y, z)]
+        return remote(here, here, csend.at[0], crecv.at[n], line_dev(o))
+
+    def spread(n, o, t):
+        here = res.at[n, core, u, subs(y)]
+        return remote(here, here, dsend.at[t], drecv.at[n], plane_dev(o))
+
+    def share(n, t):
+        here = res.at[n, core] if t == 1 else res.at[n, core, u]
+        return remote(here, here, esend.at[t], erecv.at[n], (other, u))
+
+    def whole(src, send, recv):
+        return remote(src, src, send, recv, (other, u))
 
     def pair_up(n):
-        for v in range(nu):
-            own = acc[n, v * 2 + core]
-            swap(n, v).wait_recv()
-            part[n, v] = (own.astype(F32) + pair[n, v].astype(F32)).astype(BF16)
+        swap(n).wait_recv()
+        part[n] = (acc[n, core].astype(F32) + pair[n].astype(F32)).astype(BF16)
         for o in range(1, group):
             scatter(n, o).start()
 
     def plane_sum(n):
         total = part[n, u, subs(y), :].astype(F32)
+        whole(plane_in.at[n], asend.at[0], arecv.at[n]).wait_recv()
         for o in range(1, group):
-            scatter(n, o).wait_recv()
-            total = total + plane_in[n, o].astype(F32)
+            total = total + plane_in[n, o - 1].astype(F32)
         line[n] = total.astype(BF16)
         for o in range(1, outers):
             pass_on(n, o).start()
 
     def line_sum(n):
         total = line[n, pl.ds(pl.multiple_of(z * piece, piece), piece), :].astype(F32)
+        whole(line_in.at[n], bsend.at[0], brecv.at[n]).wait_recv()
         for o in range(1, outers):
-            pass_on(n, o).wait_recv()
-            total = total + line_in[n, o].astype(F32)
-        res[n, u * 2 + core, piece_at(y, z), :] = total.astype(BF16)
+            total = total + line_in[n, o - 1].astype(F32)
+        res[n, core, u, piece_at(y, z), :] = total.astype(BF16)
         for o in range(1, outers):
             along(n, o).start()
 
-    def widen(n, count):
-        for o in range(1, outers):
-            came(n, o).wait_recv()
-        for o in range(1, count):
-            spread(n, o).start()
-        share(n, 0).start()
-
-    def hand_over(n, count):
-        for o in range(1, count):
-            landed(n, o).wait_recv()
-            share(n, o).start()
+    def widen(n, t):
+        whole(line_in.at[n], csend.at[0], crecv.at[n]).wait_recv()
+        for o in range(1, (inners, group)[t]):
+            spread(n, o, t).start()
+
+    def hand_over(n, t):
+        whole(plane_in.at[n, pl.ds(0, (inners, group)[t] - 1)], dsend.at[t], drecv.at[n]).wait_recv()
+        share(n, t).start()
 
     def each(first, stop, work):
         @pl.loop(first, stop)
@@ -852,43 +835,35 @@
     def _():
         pl.semaphore_wait(barrier, 3 * nu - 1 + group + outers - 2)
 
-    bufs = (kbuf, vbuf)
-
-    def across(a, j, c):
-        src = key_base.at[:, cols(c)] if a == 0 else vbuf.at[mine, cols(c)]
-        return pltpu.make_async_remote_copy(
-            src_ref=src, dst_ref=bufs[a].at[mine, cols(c)],
-            send_sem=xsend.at[a, j, c], recv_sem=xrecv.at[a, j, c],
-            device_id=(blk, peer(j)), device_id_type=MESH,
-        )
-
-    def crossed(a, j, c):
-        here = bufs[a].at[pl.ds(pl.multiple_of(span + source(j) * rows, rows), rows), cols(c)]
-        return pltpu.make_async_remote_copy(
-            src_ref=here, dst_ref=here,
-            send_sem=xsend.at[a, j, c], recv_sem=xrecv.at[a, j, c],
-            device_id=(blk, peer(j)), device_id_type=MESH,
-        )
-
-    def onward(a, j, c):
-        s = source(j)
-        if a == 0 and j == 0:
-            src = key_base.at[:, cols(c)]
-        else:
-            src = bufs[a].at[pl.ds(pl.multiple_of(span + s * rows, rows), rows), cols(c)]
-        return pltpu.make_async_remote_copy(
-            src_ref=src, dst_ref=bufs[a].at[pl.ds(pl.multiple_of(s * rows, rows), rows), cols(c)],
-            send_sem=fsend.at[a, j, c], recv_sem=frecv.at[a, j, c],
-            device_id=(blk + 1, u), device_id_type=MESH,
-        )
-
-    def arrived(a, j, c):
-        here = bufs[a].at[pl.ds(pl.multiple_of(source(j) * rows, rows), rows), cols(c)]
-        return pltpu.make_async_remote_copy(
-            src_ref=here, dst_ref=here,
-            send_sem=fsend.at[a, j, c], recv_sem=frecv.at[a, j, c],
-            device_id=(blk, peer(1)), device_id_type=MESH,
-        )
+    def rows_of(first, j):
+        return pl.ds(pl.multiple_of(first + source(j) * rows, rows), rows)
+
+    def cross(j, c, what):
+        at = cols(c)
+        src, dst = {
+            0: (key_base.at[:, at], kv.at[0, mine, at]),
+            1: (kv.at[1, mine, at], kv.at[1, mine, at]),
+            2: (kv.at[:, mine, at], kv.at[:, mine, at]),
+        }[what]
+        return remote(src, dst, xsend.at[j], xrecv.at[j, c], (blk, peer(j)))
+
+    def crossed(j, c):
+        here = kv.at[:, rows_of(span, j), cols(c)]
+        return remote(here, here, xsend.at[j], xrecv.at[j, c], (blk, peer(j)))
+
+    def onward(j, c, what):
+        at = cols(c)
+        old, new = rows_of(span, j), rows_of(0, j)
+        src, dst = {
+            0: (key_base.at[:, at], kv.at[0, new, at]),
+            1: (kv.at[1, old, at], kv.at[1, new, at]),
+            2: (kv.at[:, old, at], kv.at[:, new, at]),
+        }[what]
+        return remote(src, dst, fsend.at[j], frecv.at[c], (blk + 1, u))
+
+    def arrived(c):
+        here = kv.at[:, pl.ds(0, span), cols(c)]
+        return remote(here, here, fsend.at[0], frecv.at[c], (blk, peer(1)))
 
     def low_across(j):
         return pltpu.make_async_remote_copy(
@@ -924,12 +899,12 @@
     ahead = min(2048 // CHUNK, chunks)
     for c in range(early):
         for j in range(1, nu):
-            across(0, j, c).start()
+            cross(j, c, 0).start()
 
     @pl.when(has_next)
     def _():
         for c in range(ahead):
-            onward(0, 0, c).start()
+            onward(0, c, 0).start()
 
     lane = lax.broadcasted_iota(jnp.int32, (rows, 2 * rank), 1)
     for i in range(3):
@@ -938,7 +913,7 @@
     low_qm = jnp.where(lane < rank, low, 0.0).astype(BF16)
     low_vm = jnp.where(lane >= rank, low, 0.0).astype(BF16)
     lbuf[mine, :] = low_vm
-    for i in range(3, 6):
+    for i in range(3, 7):
         local[i].wait()
 
     @pl.loop(0, chunks)
@@ -953,20 +928,21 @@
     def _():
         low_onward(0).start()
 
-    @pl.loop(0, chunks)
+    @pl.loop(0, early)
     def _(c):
-        @pl.when(c >= early)
-        def _():
-            for j in range(1, nu):
-                across(0, j, c).start()
-
         for j in range(1, nu):
-            across(1, j, c).start()
+            cross(j, c, 1).start()
 
     @pl.when(has_next)
     def _():
-        for c in range(ahead):
-            onward(1, 0, c).start()
+        @pl.loop(0, ahead)
+        def _(c):
+            onward(0, c, 1).start()
+
+    @pl.loop(early, chunks)
+    def _(c):
+        for j in range(1, nu):
+            cross(j, c, 2).start()
 
     lrq[...] = jnp.zeros_like(lrq)
     lrv[...] = jnp.zeros_like(lrv)
@@ -977,7 +953,7 @@
         vbuf[pl.ds(0, span), :] = jnp.zeros((span, width), BF16)
         lbuf[pl.ds(0, span), :] = jnp.zeros((span, 2 * rank), BF16)
 
-    for i in range(6, 9):
+    for i in range(7, 9):
         local[i].wait()
 
     scale = HEAD ** (-0.5)
@@ -1013,7 +989,8 @@
             h = first + i
             att_ref[:, pl.ds(pl.multiple_of(h * HEAD, HEAD), HEAD)] = attended
             row = pl.multiple_of((offset + i) * 2 * rank, 2 * rank)
-            acc[c // cells, lax.rem(c, cells), pl.ds(row, 2 * rank), :] = gup
+            cell = lax.rem(c, cells)
+            acc[c // cells, lax.rem(cell, 2), cell // 2, pl.ds(row, 2 * rank), :] = gup
         lrq[...] += jnp.where(lane < rank, sum(r[2] for r in results), 0.0)
         lrv[...] += sum(r[3] for r in results)
 
@@ -1022,7 +999,7 @@
 
     def att_copy(c):
         return pltpu.make_async_copy(
-            att_ref.at[:, cols(c)], att_out.at[:, cols(c)], att_sem.at[c]
+            att_ref.at[:, cols(c)], att_out.at[:, cols(c)], att_sem.at[0]
         )
 
     @pl.loop(0, chunks + 1)
@@ -1043,18 +1020,16 @@
 
         @pl.when(c < chunks)
         def _():
-            for a in range(2):
-                for j in range(1, nu):
-                    crossed(a, j, c).wait_recv()
-
-                    @pl.when(has_next)
-                    def _():
-                        onward(a, j, c).start()
+            for j in range(1, nu):
+                crossed(j, c).wait_recv()
+
+                @pl.when(has_next)
+                def _():
+                    onward(j, c, 2).start()
 
             @pl.when(jnp.logical_and(has_next, c + ahead < chunks))
             def _():
-                for a in range(2):
-                    onward(a, 0, c + ahead).start()
+                onward(0, c + ahead, 2).start()
 
         @pl.when(c == chunks - 1)
         def _():
@@ -1064,20 +1039,17 @@
         def _():
             @pl.when(has_prev)
             def _():
-                for a in range(2):
-                    for j in range(nu):
-                        arrived(a, j, c - 1).wait_recv()
+                arrived(c - 1).wait_recv()
 
             @pl.loop(0, heads // together)
             def _(i):
                 head_group(c - 1, i * together)
 
             att_copy(c - 1).start()
-            cell = lax.rem(c - 1, cells)
-
-            @pl.when(lax.rem(cell, 2) != core)
+
+            @pl.when(lax.rem(c, cells) == 0)
             def _():
-                swap((c - 1) // cells, cell // 2).start()
+                swap(c // cells - 1).start()
 
     def terms(k, j, base):
         s = peer(j)
@@ -1112,70 +1084,65 @@
 
     lows = lrq[...].T.astype(BF16)
 
-    def terms_of(p, r):
-        at = pl.ds(pl.multiple_of((r * parts + p) * CHUNK, CHUNK), CHUNK)
+    def terms_of(p, v, k):
+        at = pl.ds(pl.multiple_of(((v * 2 + k) * parts + p) * CHUNK, CHUNK), CHUNK)
         block = dot(lows, tok[:, at]).astype(BF16)
         for i in range(heads):
-            acc[parts + p, r, pl.ds(i * 2 * rank, 2 * rank), :] = block[:, i * HEAD:(i + 1) * HEAD]
+            acc[parts + p, k, v, pl.ds(i * 2 * rank, 2 * rank), :] = block[:, i * HEAD:(i + 1) * HEAD]
 
     def project(p):
         for v in range(nu):
-            terms_of(p, v * 2 + 1 - core)
-            swap(parts + p, v).start()
+            terms_of(p, v, 1 - core)
+        swap(parts + p).start()
         for v in range(nu):
-            terms_of(p, v * 2 + core)
-
-    def lay_out(n, count, outs, base):
-        for o in range(count):
-            shared(n, o).wait_recv()
-        for r in range(cells if count == group else 2):
-            for i in range(heads):
-                h = (r * parts + n - base) * heads + i
-                at = pl.ds(pl.multiple_of(h * HEAD, HEAD), HEAD)
-                cell = r if count == group else u * 2 + r
-                outs[0][:, at] = res[n, cell, pl.ds(i * 2 * rank, rank), :]
-                outs[1][:, at] = res[n, cell, pl.ds(i * 2 * rank + rank, rank), :]
+            terms_of(p, v, core)
+
+    def lay_out(n, t, outs):
+        shared_here = res.at[n, 1 - core] if t == 1 else res.at[n, 1 - core, u]
+        whole(shared_here, esend.at[t], erecv.at[n]).wait_recv()
+        for v in range(nu if t == 1 else 1):
+            for k in range(2):
+                for i in range(heads):
+                    h = ((v * 2 + k) * parts + n - t * parts) * heads + i
+                    at = pl.ds(pl.multiple_of(h * HEAD, HEAD), HEAD)
+                    w = v if t == 1 else u
+                    outs[0][:, at] = res[n, k, w, pl.ds(i * 2 * rank, rank), :]
+                    outs[1][:, at] = res[n, k, w, pl.ds(i * 2 * rank + rank, rank), :]
 
     each(0, parts, project)
     each(parts, 2 * parts, pair_up)
     each(soon, parts, plane_sum)
     each(0, parts, line_sum)
     each(parts, 2 * parts, plane_sum)
-    each(0, parts, lambda n: widen(n, inners))
+    each(0, parts, lambda n: widen(n, 0))
     each(parts, 2 * parts, line_sum)
-    each(0, parts, lambda n: hand_over(n, inners))
-    each(parts, 2 * parts, lambda n: widen(n, group))
-    each(0, parts, lambda n: lay_out(n, inners, (upq_out, upv_out), 0))
-    each(parts, 2 * parts, lambda n: hand_over(n, group))
-    each(parts, 2 * parts, lambda n: lay_out(n, group, (downq_out, downv_out), parts))
-
-    def drain(n, count):
-        for v in range(nu):
-            swap(n, v).wait_send()
-        for o in range(1, group):
-            scatter(n, o).wait_send()
-        for o in range(1, outers):
-            pass_on(n, o).wait_send()
-            along(n, o).wait_send()
-        for o in range(1, count):
-            spread(n, o).wait_send()
-        for o in range(count):
-            share(n, o).wait_send()
-
-    each(0, parts, lambda n: drain(n, inners))
-    each(parts, 2 * parts, lambda n: drain(n, group))
-    each(0, chunks, lambda c: att_copy(c).wait())
-
-    @pl.loop(0, chunks)
-    def _(c):
-        for a in range(2):
-            for j in range(1, nu):
-                across(a, j, c).wait_send()
-
-            @pl.when(has_next)
-            def _():
-                for j in range(nu):
-                    onward(a, j, c).wait_send()
+    each(0, parts, lambda n: hand_over(n, 0))
+    each(parts, 2 * parts, lambda n: widen(n, 1))
+    each(0, parts, lambda n: lay_out(n, 0, (upq_out, upv_out)))
+    each(parts, 2 * parts, lambda n: hand_over(n, 1))
+    each(parts, 2 * parts, lambda n: lay_out(n, 1, (downq_out, downv_out)))
+
+    whole(pair, psend.at[0], precv.at[0]).wait_send()
+    whole(plane_in, asend.at[0], arecv.at[0]).wait_send()
+    whole(line_in, bsend.at[0], brecv.at[0]).wait_send()
+    whole(line_in, csend.at[0], crecv.at[0]).wait_send()
+    for i in range(2):
+        some = pl.ds(i * parts, parts)
+        whole(
+            plane_in.at[some, pl.ds(0, (inners, group)[i] - 1)], dsend.at[i], drecv.at[0]
+        ).wait_send()
+    whole(res.at[pl.ds(0, parts), 0, 0], esend.at[0], erecv.at[0]).wait_send()
+    whole(res.at[pl.ds(parts, parts), 0], esend.at[1], erecv.at[0]).wait_send()
+    pltpu.make_async_copy(att_ref, att_out, att_sem.at[0]).wait()
+
+    everything = kv.at[:, mine, :]
+    for j in range(1, nu):
+        remote(everything, everything, xsend.at[j], xrecv.at[j, 0], (blk, peer(j))).wait_send()
+
+    @pl.when(has_next)
+    def _():
+        for j in range(nu):
+            remote(everything, everything, fsend.at[j], frecv.at[0], (blk + 1, u)).wait_send()
 
     for j in range(1, nu):
         low_across(j).wait_send()
@@ -1226,8 +1193,7 @@
         in_specs=[anywhere] * 9,
         out_specs=(anywhere, here, here, here, here),
         scratch_shapes=[
-            pltpu.VMEM((2 * span, width), BF16),
-            pltpu.VMEM((2 * span, width), BF16),
+            pltpu.VMEM((2, 2 * span, width), BF16),
             pltpu.VMEM((2 * span, lanes), BF16),
             pltpu.VMEM((rows, width), BF16),
             pltpu.VMEM((rows, width), BF16),
@@ -1238,24 +1204,24 @@
             pltpu.VMEM((2 * span, lanes), F32),
             pltpu.VMEM((2, nu, rows, lanes), F32),
             pltpu.VMEM((rows, width), BF16),
-            pltpu.VMEM((2 * parts, cells, CHUNK, lanes), BF16),
+            pltpu.VMEM((2 * parts, 2, nu, CHUNK, lanes), BF16),
             pltpu.VMEM((2 * parts, nu, CHUNK, lanes), BF16),
             pltpu.VMEM((2 * parts, nu, CHUNK, lanes), BF16),
-            pltpu.VMEM((2 * parts, group, sub, lanes), BF16),
+            pltpu.VMEM((2 * parts, group - 1, sub, lanes), BF16),
             pltpu.VMEM((2 * parts, sub, lanes), BF16),
-            pltpu.VMEM((2 * parts, outers, sub // outers, lanes), BF16),
-            pltpu.VMEM((2 * parts, cells, CHUNK, lanes), BF16),
-            dma((9,)), dma((chunks,)),
-            dma((2, nu, chunks)), dma((2, nu, chunks)),
-            dma((2, nu, chunks)), dma((2, nu, chunks)),
+            pltpu.VMEM((2 * parts, outers - 1, sub // outers, lanes), BF16),
+            pltpu.VMEM((2 * parts, 2, nu, CHUNK, lanes), BF16),
+            dma((9,)), dma((1,)),
+            dma((nu,)), dma((nu, chunks)),
+            dma((nu,)), dma((chunks,)),
             dma((nu,)), dma((nu,)), dma((nu,)), dma((nu,)),
             dma((2, nu)), dma((2, nu)),
-            dma((2 * parts, nu)), dma((2 * parts, nu)),
-            dma((2 * parts, group)), dma((2 * parts, group)),
-            dma((2 * parts, outers)), dma((2 * parts, outers)),
-            dma((2 * parts, outers)), dma((2 * parts, outers)),
-            dma((2 * parts, group)), dma((2 * parts, group)),
-            dma((2 * parts, group)), dma((2 * parts, group)),
+            dma((1,)), dma((2 * parts,)),
+            dma((1,)), dma((2 * parts,)),
+            dma((1,)), dma((2 * parts,)),
+            dma((1,)), dma((2 * parts,)),
+            dma((2,)), dma((2 * parts,)),
+            dma((2,)), dma((2 * parts,)),
         ],
         compiler_params=pltpu.CompilerParams(
             collective_id=2, has_side_effects=True, vmem_limit_bytes=65_000_000

time: 122 us -> 115 us (0.943)
  Pallas kernels: 115 us -> 108 us
    pallas_call x1, Pallas kernels: 115 us -> 108 us  [fused(): pl.pallas_call(functools.partial(fused_kernel, nb, nu), out_shape=(jax.Sh...]
where the time goes in v3:
time: 115 us
  Pallas kernels  108 us (94%)
  local copies, waits for them, and re-layouts  5.95 us (5%)
    pallas_call x1, Pallas kernels, fused(): pl.pallas_call(functools.partial(fused_kernel, nb, nu), out_shape=(jax.Sh...  108 us
    unnamed x13, local copies, waits for them, and re-layouts  5.95 us

profile of v3, /device:TPU:9, one launch (start us, length us, event | category | flops | bytes accessed | tf_op | source)
XLA Modules:
  0.0 115.0 jit_solution(1862203171613302229)
XLA Ops:
  0.6 108.3 %shard_map.128 = (bf16[128,5120]{1,0:T(8,128)(2,1)}, bf16[64,5120]{1,0:T(8,128)(2,1)}, bf16[64,5120]{1,0:T(8,128)(2,1)}, bf16[64,2560]{1,0:T(8,128)(2,1)}, bf16[64,2560]{1,0:T(8,128)(2,1)}) custom-call(bf16[128,5120]{1,0:T(8,128)(2,1)} %tokens.1, bf16[128,5120]{1,0:T(8,128)(2,1)} %query_base.1, bf16[128,5120]{1,0:T(8,128)(2,1)} %key_base.1, ...), custom_call_target="tpu_custom_call" | custom-call | tf_op jit(solution)/shard_map/pallas_call | solution.py:1184
  109.0 0.0 copy-start.1
  109.0 2.5 %copy.19 = bf16[128,5120]{1,0:T(8,128)(2,1)} copy(bf16[128,5120]{1,0:T(8,128)(2,1)} %get-tuple-element.20) | data formatting | bytes 2621440
  111.5 0.0 copy-done.1
  111.5 0.0 copy-start.3
  111.5 0.0 copy-start
  111.5 0.0 copy-start.2
  111.5 0.8 copy.20
  112.4 0.3 copy-done.3
  112.7 0.7 copy.21
  113.4 0.0 copy-done
  113.4 0.8 copy.22
  114.2 0.0 copy-done.2
  114.2 0.7 copy.23
Async XLA Ops:
  109.0 2.5 %copy-start.1 = (bf16[64,5120]{1,0:T(8,128)(2,1)S(1)}, bf16[64,5120]{1,0:T(8,128)(2,1)}, u32[]{:S(2)}) copy-start(bf16[64,5120]{1,0:T(8,128)(2,1)} %get-tuple-element.11) | copy-start | bytes 1966084
  111.5 1.1 copy-start.3
  111.5 1.9 %copy-start = (bf16[64,5120]{1,0:T(8,128)(2,1)S(1)}, bf16[64,5120]{1,0:T(8,128)(2,1)}, u32[]{:S(2)}) copy-start(bf16[64,5120]{1,0:T(8,128)(2,1)} %get-tuple-element.13) | copy-start | bytes 1966084
  111.5 2.7 %copy-start.2 = (bf16[64,2560]{1,0:T(8,128)(2,1)S(1)}, bf16[64,2560]{1,0:T(8,128)(2,1)}, u32[]{:S(2)}) copy-start(bf16[64,2560]{1,0:T(8,128)(2,1)} %get-tuple-element.24) | copy-start | bytes 983044

commit v4 on v3

--- a/solution.py
+++ b/solution.py
@@ -650,10 +650,10 @@
 def fused_kernel(
     nb, nu,
     tokens, query_base, key_base, value_base, out_grad, down_q, up_q, down_v, up_v,
-    att_out, downq_out, downv_out, upq_out, upv_out,
-    kv, lbuf, tok, qs, gs, downs, ups, lrq, lrv, lrin, att_ref,
+    att_ref, downq_out, downv_out, upq_out, upv_out,
+    kv, lbuf, tok, qs, gs, downs, ups, lrq, lrv, lrin,
     acc, pair, part, plane_in, line, line_in, res,
-    local_sem, att_sem, xsend, xrecv, fsend, frecv, lsend, lrecv, msend, mrecv, rsend, rrecv,
+    local_sem, xsend, xrecv, fsend, frecv, lsend, lrecv, msend, mrecv, rsend, rrecv,
     psend, precv, asend, arecv, bsend, brecv, csend, crecv, dsend, drecv, esend, erecv,
 ):
     kbuf, vbuf = kv.at[0], kv.at[1]
@@ -997,11 +997,6 @@
     heads = CHUNK // HEAD
     soon = max(parts - 2, 0)
 
-    def att_copy(c):
-        return pltpu.make_async_copy(
-            att_ref.at[:, cols(c)], att_out.at[:, cols(c)], att_sem.at[0]
-        )
-
     @pl.loop(0, chunks + 1)
     def _(c):
         @pl.when(c == 0)
@@ -1045,7 +1040,6 @@
             def _(i):
                 head_group(c - 1, i * together)
 
-            att_copy(c - 1).start()
 
             @pl.when(lax.rem(c, cells) == 0)
             def _():
@@ -1133,7 +1127,6 @@
         ).wait_send()
     whole(res.at[pl.ds(0, parts), 0, 0], esend.at[0], erecv.at[0]).wait_send()
     whole(res.at[pl.ds(parts, parts), 0], esend.at[1], erecv.at[0]).wait_send()
-    pltpu.make_async_copy(att_ref, att_out, att_sem.at[0]).wait()
 
     everything = kv.at[:, mine, :]
     for j in range(1, nu):
@@ -1184,14 +1177,14 @@
     return pl.pallas_call(
         functools.partial(fused_kernel, nb, nu),
         out_shape=(
-            jax.ShapeDtypeStruct((rows, width), BF16),
-            jax.ShapeDtypeStruct((rank, width), BF16),
-            jax.ShapeDtypeStruct((rank, width), BF16),
-            jax.ShapeDtypeStruct((rank, width // nu), BF16),
-            jax.ShapeDtypeStruct((rank, width // nu), BF16),
+            pltpu.VMEM((rows, width), BF16),
+            pltpu.VMEM((rank, width), BF16),
+            pltpu.VMEM((rank, width), BF16),
+            pltpu.VMEM((rank, width // nu), BF16),
+            pltpu.VMEM((rank, width // nu), BF16),
         ),
         in_specs=[anywhere] * 9,
-        out_specs=(anywhere, here, here, here, here),
+        out_specs=(here,) * 5,
         scratch_shapes=[
             pltpu.VMEM((2, 2 * span, width), BF16),
             pltpu.VMEM((2 * span, lanes), BF16),
@@ -1203,7 +1196,6 @@
             pltpu.VMEM((rows, lanes), F32),
             pltpu.VMEM((2 * span, lanes), F32),
             pltpu.VMEM((2, nu, rows, lanes), F32),
-            pltpu.VMEM((rows, width), BF16),
             pltpu.VMEM((2 * parts, 2, nu, CHUNK, lanes), BF16),
             pltpu.VMEM((2 * parts, nu, CHUNK, lanes), BF16),
             pltpu.VMEM((2 * parts, nu, CHUNK, lanes), BF16),
@@ -1211,7 +1203,7 @@
             pltpu.VMEM((2 * parts, sub, lanes), BF16),
             pltpu.VMEM((2 * parts, outers - 1, sub // outers, lanes), BF16),
             pltpu.VMEM((2 * parts, 2, nu, CHUNK, lanes), BF16),
-            dma((9,)), dma((1,)),
+            dma((9,)),
             dma((nu,)), dma((nu, chunks)),
             dma((nu,)), dma((chunks,)),
             dma((nu,)), dma((nu,)), dma((nu,)), dma((nu,)),
@@ -1224,7 +1216,7 @@
             dma((2,)), dma((2 * parts,)),
         ],
         compiler_params=pltpu.CompilerParams(
-            collective_id=2, has_side_effects=True, vmem_limit_bytes=65_000_000
+            collective_id=2, has_side_effects=True, vmem_limit_bytes=60_000_000
         ),
     )(*operands)
 
@@ -1239,10 +1231,30 @@
     )
 
 
+def deliver_kernel(*refs):
+    count = len(refs) // 2
+    sources, targets, sem = refs[:count], refs[count:2 * count], refs[-1]
+    copies = [pltpu.make_async_copy(a, b, sem.at[i]) for i, (a, b) in enumerate(zip(sources, targets))]
+    for copy in copies:
+        copy.start()
+    for copy in copies:
+        copy.wait()
+
+
+def deliver(*arrays):
+    return pl.pallas_call(
+        deliver_kernel,
+        out_shape=tuple(jax.ShapeDtypeStruct(a.shape, a.dtype) for a in arrays),
+        in_specs=[pl.BlockSpec(memory_space=pl.ANY)] * len(arrays),
+        out_specs=tuple(pl.BlockSpec(memory_space=pl.ANY) for _ in arrays),
+        scratch_shapes=[pltpu.SemaphoreType.DMA((len(arrays),))],
+    )(*(pltpu.with_memory_space_constraint(a, pltpu.VMEM) for a in arrays))
+
+
 def per_device(nb, nu, tokens, query_base, key_base, value_base, out_grad, down_q, up_q, down_v, up_v):
     operands = (tokens, query_base, key_base, value_base, out_grad, down_q.T, up_q, down_v.T, up_v)
     if fits(nb, nu, *tokens.shape, up_q.shape[0]):
-        attended, grad_down_q, grad_down_v, grad_up_q, grad_up_v = fused(nb, nu, *operands)
+        attended, grad_down_q, grad_down_v, grad_up_q, grad_up_v = deliver(*fused(nb, nu, *operands))
         return attended, grad_down_q.T, grad_up_q, grad_down_v.T, grad_up_v
     attended, gup, lowrank = attention(nb, nu, *operands)
     grad_down_q, grad_down_v, grad_up_q, grad_up_v = reduction(nb, nu, tokens, lowrank, gup)

time: 115 us -> 110 us (0.957)
  local copies, waits for them, and re-layouts: 5.95 us -> 0 us
    unnamed x13 -> x0, local copies, waits for them, and re-layouts: 5.95 us -> none
    pallas_call x1 -> x2, Pallas kernels: 108 us -> 109 us  [the longest x1 107 us: fused(): pl.pallas_call(functools.partial(fused_kernel, nb, nu), out_shape=(pltpu....]
where the time goes in v4:
time: 110 us; the launch traced here: 109 us
  Pallas kernels  109 us (99%)
    pallas_call x1, Pallas kernels, fused(): pl.pallas_call(functools.partial(fused_kernel, nb, nu), out_shape=(pltpu....  107 us

profile of v4, /device:TPU:9, one launch (start us, length us, event | category | flops | bytes accessed | tf_op | source)
XLA Modules:
  0.0 109.5 jit_solution(11912795644622814424)
XLA Ops:
  0.6 107.1 %shard_map.128 = (bf16[128,5120]{1,0:T(8,128)(2,1)S(1)}, bf16[64,5120]{1,0:T(8,128)(2,1)S(1)}, bf16[64,5120]{1,0:T(8,128)(2,1)S(1)}, bf16[64,2560]{1,0:T(8,128)(2,1)S(1)}, bf16[64,2560]{1,0:T(8,128)(2,1)S(1)}) custom-call(bf16[128,5120]{1,0:T(8,128)(2,1)} %tokens.1, bf16[128,5120]{1,0:T(8,128)(2,1)} %query_base.1, bf16[128,5120]{1,0:T(8,128)(2,1)} %key_base.1, ...), custom_call_target="tpu_custom_call" | custom-call | tf_op jit(solution)/shard_map/pallas_call | solution.py:1177
  107.7 1.7 %shard_map.129 = (bf16[128,5120]{1,0:T(8,128)(2,1)}, bf16[64,5120]{1,0:T(8,128)(2,1)}, bf16[64,5120]{1,0:T(8,128)(2,1)}, bf16[64,2560]{1,0:T(8,128)(2,1)}, bf16[64,2560]{1,0:T(8,128)(2,1)}) custom-call(bf16[128,5120]{1,0:T(8,128)(2,1)S(1)} %get-tuple-element.15.refs_0_, bf16[64,5120]{1,0:T(8,128)(2,1)S(1)} %get-tuple-element.16.refs_1_, ...), custom_call_target="tpu_custom_call" | custom-call | tf_op jit(solution)/shard_map/pallas_call | solution.py:1245

commit v5 on v4

--- a/solution.py
+++ b/solution.py
@@ -651,10 +651,10 @@
     nb, nu,
     tokens, query_base, key_base, value_base, out_grad, down_q, up_q, down_v, up_v,
     att_ref, downq_out, downv_out, upq_out, upv_out,
-    kv, lbuf, tok, qs, gs, downs, ups, lrq, lrv, lrin,
-    acc, pair, part, plane_in, line, line_in, res,
+    kv, lbuf, tok, qs, gs, downs, ups, lrq, lrv, lrs, lrin,
+    tok2, lowb, acc, pair, part, plane_in, line, line_in, res,
     local_sem, xsend, xrecv, fsend, frecv, lsend, lrecv, msend, mrecv, rsend, rrecv,
-    psend, precv, asend, arecv, bsend, brecv, csend, crecv, dsend, drecv, esend, erecv,
+    psend, precv, asend, arecv, bsend, brecv, csend, crecv, dsend, drecv, esend, erecv, gsend, grecv,
 ):
     kbuf, vbuf = kv.at[0], kv.at[1]
     blk = lax.axis_index("blk")
@@ -754,6 +754,17 @@
     def whole(src, send, recv):
         return remote(src, src, send, recv, (other, u))
 
+    strip = parts * CHUNK
+
+    def lend(v):
+        at = pl.ds(pl.multiple_of((v * 2 + 1 - core) * strip, strip), strip)
+        return remote(
+            tokens.at[:, at], tok2.at[:, pl.ds(v * strip, strip)], gsend.at[0], grecv.at[0], (other, u)
+        )
+
+    def tell():
+        return remote(lowb.at[0], lowb.at[1], gsend.at[1], grecv.at[1], (other, u))
+
     def pair_up(n):
         swap(n).wait_recv()
         part[n] = (acc[n, core].astype(F32) + pair[n].astype(F32)).astype(BF16)
@@ -895,8 +906,8 @@
             device_id=(blk, peer(1)), device_id_type=MESH,
         )
 
-    early = min(3 * 512 // CHUNK, chunks)
-    ahead = min(2048 // CHUNK, chunks)
+    early = min(2, chunks)
+    ahead = min(4, chunks)
     for c in range(early):
         for j in range(1, nu):
             cross(j, c, 0).start()
@@ -905,6 +916,9 @@
     def _():
         for c in range(ahead):
             onward(0, c, 0).start()
+
+    for v in range(nu):
+        lend(v).start()
 
     lane = lax.broadcasted_iota(jnp.int32, (rows, 2 * rank), 1)
     for i in range(3):
@@ -916,10 +930,9 @@
     for i in range(3, 7):
         local[i].wait()
 
-    @pl.loop(0, chunks)
-    def _(c):
-        part = dot(low_vm, ups[:, cols(c)])
-        vbuf[mine, cols(c)] = (vbuf[mine, cols(c)].astype(F32) + part).astype(BF16)
+    def lift(c):
+        extra = dot(low_vm, ups[:, cols(c)])
+        vbuf[mine, cols(c)] = (vbuf[mine, cols(c)].astype(F32) + extra).astype(BF16)
 
     for j in range(1, nu):
         low_across(j).start()
@@ -930,8 +943,15 @@
 
     @pl.loop(0, early)
     def _(c):
+        lift(c)
         for j in range(1, nu):
             cross(j, c, 1).start()
+
+    @pl.loop(early, ahead)
+    def _(c):
+        lift(c)
+        for j in range(1, nu):
+            cross(j, c, 2).start()
 
     @pl.when(has_next)
     def _():
@@ -939,8 +959,9 @@
         def _(c):
             onward(0, c, 1).start()
 
-    @pl.loop(early, chunks)
+    @pl.loop(ahead, chunks)
     def _(c):
+        lift(c)
         for j in range(1, nu):
             cross(j, c, 2).start()
 
@@ -995,11 +1016,24 @@
         lrv[...] += sum(r[3] for r in results)
 
     heads = CHUNK // HEAD
-    soon = max(parts - 2, 0)
+    soon = max(parts - 1, 0)
 
     @pl.loop(0, chunks + 1)
     def _(c):
-        @pl.when(c == 0)
+        @pl.when(c < chunks)
+        def _():
+            for j in range(1, nu):
+                crossed(j, c).wait_recv()
+
+                @pl.when(has_next)
+                def _():
+                    onward(j, c, 2).start()
+
+            @pl.when(jnp.logical_and(has_next, c + ahead < chunks))
+            def _():
+                onward(0, c + ahead, 2).start()
+
+        @pl.when(c == 1)
         def _():
             for j in range(1, nu):
                 low_crossed(j).wait_recv()
@@ -1012,19 +1046,6 @@
             def _():
                 for j in range(nu):
                     low_arrived(j).wait_recv()
-
-        @pl.when(c < chunks)
-        def _():
-            for j in range(1, nu):
-                crossed(j, c).wait_recv()
-
-                @pl.when(has_next)
-                def _():
-                    onward(j, c, 2).start()
-
-            @pl.when(jnp.logical_and(has_next, c + ahead < chunks))
-            def _():
-                onward(0, c + ahead, 2).start()
 
         @pl.when(c == chunks - 1)
         def _():
@@ -1045,10 +1066,12 @@
             def _():
                 swap(c // cells - 1).start()
 
+    lrs[...] = lrv[...].astype(BF16)
+
     def terms(k, j, base):
         s = peer(j)
         return pltpu.make_async_remote_copy(
-            src_ref=lrv.at[pl.ds(pl.multiple_of(base + s * rows, rows), rows)],
+            src_ref=lrs.at[pl.ds(pl.multiple_of(base + s * rows, rows), rows)],
             dst_ref=lrin.at[k, j],
             send_sem=rsend.at[k, j], recv_sem=rrecv.at[k, j],
             device_id=(blk - k, s), device_id_type=MESH,
@@ -1068,28 +1091,26 @@
     lrq[...] += lrv[mine, :]
     for j in range(1, nu):
         terms(0, j, span).wait_recv()
-        lrq[...] += lrin[0, j]
+        lrq[...] += lrin[0, j].astype(F32)
 
     @pl.when(has_next)
     def _():
         for j in range(nu):
             terms(1, j, 0).wait_recv()
-            lrq[...] += lrin[1, j]
-
-    lows = lrq[...].T.astype(BF16)
-
-    def terms_of(p, v, k):
-        at = pl.ds(pl.multiple_of(((v * 2 + k) * parts + p) * CHUNK, CHUNK), CHUNK)
-        block = dot(lows, tok[:, at]).astype(BF16)
-        for i in range(heads):
-            acc[parts + p, k, v, pl.ds(i * 2 * rank, 2 * rank), :] = block[:, i * HEAD:(i + 1) * HEAD]
+            lrq[...] += lrin[1, j].astype(F32)
+
+    lowb[0] = lrq[...].T.astype(BF16)
+    tell().start()
 
     def project(p):
         for v in range(nu):
-            terms_of(p, v, 1 - core)
-        swap(parts + p).start()
-        for v in range(nu):
-            terms_of(p, v, core)
+            at = pl.ds(pl.multiple_of((v * 2 + core) * strip + p * CHUNK, CHUNK), CHUNK)
+            there = pl.ds(pl.multiple_of(v * strip + p * CHUNK, CHUNK), CHUNK)
+            block = (dot(lowb[0], tok[:, at]) + dot(lowb[1], tok2[:, there])).astype(BF16)
+            for i in range(heads):
+                part[parts + p, v, pl.ds(i * 2 * rank, 2 * rank), :] = block[:, i * HEAD:(i + 1) * HEAD]
+        for o in range(1, group):
+            scatter(parts + p, o).start()
 
     def lay_out(n, t, outs):
         shared_here = res.at[n, 1 - core] if t == 1 else res.at[n, 1 - core, u]
@@ -1103,19 +1124,35 @@
                     outs[0][:, at] = res[n, k, w, pl.ds(i * 2 * rank, rank), :]
                     outs[1][:, at] = res[n, k, w, pl.ds(i * 2 * rank + rank, rank), :]
 
+    whole(tok2, gsend.at[0], grecv.at[0]).wait_recv()
+    tell().wait_recv()
     each(0, parts, project)
-    each(parts, 2 * parts, pair_up)
-    each(soon, parts, plane_sum)
-    each(0, parts, line_sum)
-    each(parts, 2 * parts, plane_sum)
-    each(0, parts, lambda n: widen(n, 0))
-    each(parts, 2 * parts, line_sum)
-    each(0, parts, lambda n: hand_over(n, 0))
-    each(parts, 2 * parts, lambda n: widen(n, 1))
-    each(0, parts, lambda n: lay_out(n, 0, (upq_out, upv_out)))
-    each(parts, 2 * parts, lambda n: hand_over(n, 1))
-    each(parts, 2 * parts, lambda n: lay_out(n, 1, (downq_out, downv_out)))
-
+
+    def finish_up(n):
+        lay_out(n, 0, (upq_out, upv_out))
+
+    def finish_down(n):
+        lay_out(n, 1, (downq_out, downv_out))
+
+    order = []
+    for p in range(parts):
+        late = 3.0 if p >= soon else 0.0
+        if p >= soon:
+            order.append((-0.5, plane_sum, (p,)))
+        order += [
+            (late, line_sum, (p,)), (3.5 + late, widen, (p, 0)),
+            (11.0 + 0.7 * p, hand_over, (p, 0)), (14.0 + 0.7 * p, finish_up, (p,)),
+        ]
+        n, at = parts + p, 1.4 * p
+        order += [
+            (2.6 + at, plane_sum, (n,)), (5.9 + at, line_sum, (n,)), (9.5 + at, widen, (n, 1)),
+            (13.3 + at, hand_over, (n, 1)), (14.5 + at, finish_down, (n,)),
+        ]
+    for _, work, what in sorted(order, key=lambda item: item[0]):
+        work(*what)
+
+    whole(tok2, gsend.at[0], grecv.at[0]).wait_send()
+    tell().wait_send()
     whole(pair, psend.at[0], precv.at[0]).wait_send()
     whole(plane_in, asend.at[0], arecv.at[0]).wait_send()
     whole(line_in, bsend.at[0], brecv.at[0]).wait_send()
@@ -1195,9 +1232,12 @@
             pltpu.VMEM((lanes, width), BF16),
             pltpu.VMEM((rows, lanes), F32),
             pltpu.VMEM((2 * span, lanes), F32),
-            pltpu.VMEM((2, nu, rows, lanes), F32),
-            pltpu.VMEM((2 * parts, 2, nu, CHUNK, lanes), BF16),
-            pltpu.VMEM((2 * parts, nu, CHUNK, lanes), BF16),
+            pltpu.VMEM((2 * span, lanes), BF16),
+            pltpu.VMEM((2, nu, rows, lanes), BF16),
+            pltpu.VMEM((rows, width // 2), BF16),
+            pltpu.VMEM((2, lanes, rows), BF16),
+            pltpu.VMEM((parts, 2, nu, CHUNK, lanes), BF16),
+            pltpu.VMEM((parts, nu, CHUNK, lanes), BF16),
             pltpu.VMEM((2 * parts, nu, CHUNK, lanes), BF16),
             pltpu.VMEM((2 * parts, group - 1, sub, lanes), BF16),
             pltpu.VMEM((2 * parts, sub, lanes), BF16),
@@ -1208,12 +1248,13 @@
             dma((nu,)), dma((chunks,)),
             dma((nu,)), dma((nu,)), dma((nu,)), dma((nu,)),
             dma((2, nu)), dma((2, nu)),
-            dma((1,)), dma((2 * parts,)),
+            dma((1,)), dma((parts,)),
             dma((1,)), dma((2 * parts,)),
             dma((1,)), dma((2 * parts,)),
             dma((1,)), dma((2 * parts,)),
             dma((2,)), dma((2 * parts,)),
             dma((2,)), dma((2 * parts,)),
+            dma((2,)), dma((2,)),
         ],
         compiler_params=pltpu.CompilerParams(
             collective_id=2, has_side_effects=True, vmem_limit_bytes=60_000_000

time: 110 us -> 104 us (0.945); the launches traced: 109 us -> 102 us
  Pallas kernels: 109 us -> 102 us
    pallas_call x1, Pallas kernels: 107 us -> 99.9 us  [fused(): pl.pallas_call(functools.partial(fused_kernel, nb, nu), out_shape=(pltpu....]
where the time goes in v5:
time: 104 us; the launch traced here: 102 us
  Pallas kernels  102 us (98%)
    pallas_call x1, Pallas kernels, fused(): pl.pallas_call(functools.partial(fused_kernel, nb, nu), out_shape=(pltpu....  99.9 us

profile of v5, /device:TPU:9, one launch (start us, length us, event | category | flops | bytes accessed | tf_op | source)
XLA Modules:
  0.0 102.3 jit_solution(16318035773909591434)
XLA Ops:
  0.6 99.9 %shard_map.128 = (bf16[128,5120]{1,0:T(8,128)(2,1)S(1)}, bf16[64,5120]{1,0:T(8,128)(2,1)S(1)}, bf16[64,5120]{1,0:T(8,128)(2,1)S(1)}, bf16[64,2560]{1,0:T(8,128)(2,1)S(1)}, bf16[64,2560]{1,0:T(8,128)(2,1)S(1)}) custom-call(bf16[128,5120]{1,0:T(8,128)(2,1)} %tokens.1, bf16[128,5120]{1,0:T(8,128)(2,1)} %query_base.1, bf16[128,5120]{1,0:T(8,128)(2,1)} %key_base.1, ...), custom_call_target="tpu_custom_call" | custom-call | tf_op jit(solution)/shard_map/pallas_call | solution.py:1214
  100.6 1.7 %shard_map.129 = (bf16[128,5120]{1,0:T(8,128)(2,1)}, bf16[64,5120]{1,0:T(8,128)(2,1)}, bf16[64,5120]{1,0:T(8,128)(2,1)}, bf16[64,2560]{1,0:T(8,128)(2,1)}, bf16[64,2560]{1,0:T(8,128)(2,1)}) custom-call(bf16[128,5120]{1,0:T(8,128)(2,1)S(1)} %get-tuple-element.15.refs_0_, bf16[64,5120]{1,0:T(8,128)(2,1)S(1)} %get-tuple-element.16.refs_1_, ...), custom_call_target="tpu_custom_call" | custom-call | tf_op jit(solution)/shard_map/pallas_call | solution.py:1286
